TPU v7x, 32 devices: a whole 2x2x4 slice. The times are simulated.
32 devices in a mesh: section: 2 (over y), dp: 4 (over x, core), expert: 4 (over z).
Axes of the slice: x: 2, y: 2, z: 4, core: 2. Of those that a mesh axis runs over, the one named last changes fastest.
Arguments:
- upstream: bfloat16 [2, 256, 4096], P('section', 'expert', 'dp'), may hold values from -6 to 6
- routes: int32 [2, 256, 2], P('section', 'expert'), may hold values from 0 to 3, all different within a row; in each aligned block of 64 rows (0 to 63, 64 to 127, ..., all dimensions but the last counted through in order) at most 48 rows name the same one
- gate_weights: bfloat16 [2, 256, 2], P('section', 'expert'), may hold values from 0.049804688 to 0.5
- w_gate: bfloat16 [2, 4, 4096, 768], P('section', 'expert', 'dp'), may hold values from -0.09375 to 0.09375
- w_up: bfloat16 [2, 4, 4096, 768], P('section', 'expert', 'dp'), may hold values from -0.09375 to 0.09375
- w_down: bfloat16 [2, 4, 768, 4096], P('section', 'expert', None, 'dp'), may hold values from -0.21875 to 0.21875
- saved_gate: bfloat16 [2, 4, 4, 48, 768], P('section', 'expert'), may hold values from -6 to 6
- saved_up: bfloat16 [2, 4, 4, 48, 768], P('section', 'expert'), may hold values from -6 to 6
Outputs:
- handed: bfloat16 [2, 256, 4096], P('section', 'expert', 'dp')
- gate_grads: bfloat16 [2, 256, 2], P('section', 'expert')
Inputs may be any that keep to these rules, and one draw needn't show every extreme that they name: `routes`: each token names 2 different experts; among the 64 tokens of one device no expert is named by more than 48 tokens, and in every draw some expert is named by exactly 48 tokens of some device.
All inputs are finite; a program needn't handle non-finite values.
Results may differ from a plain program's by a relative error of at most 0.015.
Values may be sent and summed in bfloat16 or wider, within the bound.
No kernel may reach another device: no remote copies, remote signals or barrier semaphores. Data moves between devices by JAX's collectives and lax.ppermute only.
A program may use at most 64 MiB of HBM per device.

v0:
```python
import jax
import jax.numpy as jnp
from jax import lax
from jax.sharding import PartitionSpec as P


def shifted(value, axis, steps):
    count = lax.axis_size(axis)
    initial, last = (max(0, -steps), min(count, count - steps))
    return lax.ppermute(value, axis, [(source, source + steps) for source in range(initial, last)])


def slot_tables(route_block, experts, capacity):
    tokens_here, picks_here = route_block.shape
    labels = jnp.arange(experts, dtype=jnp.int32)
    onehot = (route_block[:, :, None] == labels[None, None, :]).astype(jnp.int32)
    per_token = jnp.sum(onehot, axis=1)
    earlier = jnp.cumsum(per_token, axis=0) - per_token
    slot = jnp.sum(onehot * earlier[:, None, :], axis=2)
    target = (route_block * capacity + slot).reshape(-1)
    places = jnp.arange(experts * capacity, dtype=jnp.int32)
    placement = (places[:, None] == target[None, :]).astype(jnp.bfloat16)
    by_token = jnp.sum(placement.reshape(experts * capacity, tokens_here, picks_here), axis=2)
    return (placement, by_token)


def swiglu_back(hidden_grad, gate_pre, up_pre):
    gate_val = gate_pre.astype(jnp.float32)
    up_val = up_pre.astype(jnp.float32)
    sigmoid_val = jax.nn.sigmoid(gate_val)
    silu_val = gate_val * sigmoid_val
    gate_back = (
        hidden_grad * up_val * sigmoid_val * (1.0 + gate_val * (1.0 - sigmoid_val))
    ).astype(jnp.bfloat16)
    up_back = (hidden_grad * silu_val).astype(jnp.bfloat16)
    return (gate_back, up_back)


def per_device(upstream, routes, gate_weights, w_gate, w_up, w_down, saved_gate, saved_up):
    grads_here = upstream[0]
    route_block = routes[0]
    experts = lax.axis_size("expert")
    groups = saved_gate.shape[2]
    capacity = saved_gate.shape[3]
    slot_count = groups * capacity
    feature_width = grads_here.shape[1]
    placement, by_token = slot_tables(route_block, experts, capacity)
    send_rows = jnp.dot(by_token, grads_here, preferred_element_type=jnp.float32).astype(
        jnp.bfloat16
    )
    send_gate = jnp.dot(
        placement, gate_weights[0].reshape(-1), preferred_element_type=jnp.float32
    ).astype(jnp.bfloat16)
    recv_rows, recv_gate = (
        lax.all_to_all(
            send_rows.reshape(experts, capacity, feature_width),
            "expert",
            split_axis=0,
            concat_axis=0,
            tiled=True,
        ),
        lax.all_to_all(
            send_gate.reshape(experts, capacity), "expert", split_axis=0, concat_axis=0, tiled=True
        ),
    )
    slot_rows = recv_rows.reshape(slot_count, feature_width)
    slot_gate = recv_gate.reshape(slot_count)
    gate_pre = saved_gate[0, 0].reshape(slot_count, -1)
    up_pre = saved_up[0, 0].reshape(slot_count, -1)
    down_local = w_down[0, 0]
    scaled = (slot_gate.astype(jnp.float32)[:, None] * slot_rows.astype(jnp.float32)).astype(
        jnp.bfloat16
    )
    hidden_part = lax.dot_general(
        scaled, down_local, (((1,), (1,)), ((), ())), preferred_element_type=jnp.float32
    )
    gate_val = gate_pre.astype(jnp.float32)
    hidden = (gate_val * jax.nn.sigmoid(gate_val) * up_pre.astype(jnp.float32)).astype(jnp.bfloat16)
    expert_out = jnp.dot(hidden, down_local, preferred_element_type=jnp.float32).astype(
        jnp.bfloat16
    )
    hidden_grad = lax.psum(hidden_part.astype(jnp.bfloat16), "dp").astype(jnp.float32)
    gate_back, up_back = swiglu_back(hidden_grad, gate_pre, up_pre)
    extra_back = expert_out.reshape(groups, capacity, feature_width)
    contract = (((1,), (1,)), ((), ()))
    row_grad = (
        lax.dot_general(gate_back, w_gate[0, 0], contract, preferred_element_type=jnp.float32)
        + lax.dot_general(up_back, w_up[0, 0], contract, preferred_element_type=jnp.float32)
    ).astype(jnp.bfloat16)
    back_rows, back_extra = (
        lax.all_to_all(
            row_grad.reshape(groups, capacity, feature_width),
            "expert",
            split_axis=0,
            concat_axis=0,
            tiled=True,
        ),
        lax.all_to_all(extra_back, "expert", split_axis=0, concat_axis=0, tiled=True),
    )
    inner_back = jnp.sum(
        back_extra.reshape(slot_count, feature_width).astype(jnp.float32)
        * send_rows.astype(jnp.float32),
        axis=1,
    )
    slot_back = lax.psum(inner_back.astype(jnp.bfloat16), "dp")
    routed_sum = lax.dot_general(
        by_token,
        back_rows.reshape(slot_count, feature_width),
        (((0,), (0,)), ((), ())),
        preferred_element_type=jnp.float32,
    )
    layer_grad = (grads_here.astype(jnp.float32) + routed_sum).astype(jnp.bfloat16)
    handed = shifted(layer_grad, "section", -1)
    gate_grads = (
        jnp.dot(slot_back, placement, preferred_element_type=jnp.float32)
        .astype(jnp.bfloat16)
        .reshape(route_block.shape)
    )
    return (handed[None], gate_grads[None])


def solution(mesh):
    placed = (
        P("section", "expert", "dp"),
        P("section", "expert", None),
        P("section", "expert", None),
        P("section", "expert", "dp", None),
        P("section", "expert", "dp", None),
        P("section", "expert", None, "dp"),
        P("section", "expert", None, None, None),
        P("section", "expert", None, None, None),
    )
    return jax.shard_map(
        per_device,
        mesh=mesh,
        in_specs=placed,
        out_specs=(P("section", "expert", "dp"), P("section", "expert", None)),
        check_vma=False,
    )
```

profile of v0, /device:TPU:0, one launch (start us, length us, event | category | flops | bytes accessed | tf_op | source)
XLA Modules:
  0.0 117.4 jit_solution(11747973921744513255)
XLA Ops:
  7.2 1.4 %fusion.35 = bf16[1,1,4,48,768]{4,3,2,1,0:T(8,128)(2,1)S(1)} fusion(bf16[1,1,4,48,768]{4,3,2,1,0:T(8,128)(2,1)} %param.14, bf16[1,1,4,48,768]{4,3,2,1,0:T(8,128)(2,1)} %param.15), kind=kLoop, calls=%fused_computation.39 | loop fusion | flops 1179648 | bytes 884736 | tf_op jit(solution)/shard_map/convert_element_type | solution.py:78
  8.6 0.2 copy-done
  8.8 1.2 %fusion.14 = bf16[192,1024]{1,0:T(8,128)(2,1)} fusion(bf16[192,768]{1,0:T(8,128)(2,1)S(1)} %bitcast.76, bf16[1,1,768,1024]{3,2,1,0:T(8,128)(2,1)S(1)} %copy-done), kind=kOutput, calls=%fused_computation.10 | convolution fusion | flops 302186496 | bytes 2260992 | tf_op jit(solution)/shard_map/dot_general | solution.py:79
  10.0 6.3 %all-to-all-start.3 = ((bf16[4,48,1024]{2,1,0:T(8,128)(2,1)}), bf16[4,48,1024]{2,1,0:T(8,128)(2,1)S(1)}, u32[]{:S(2)}, u32[]{:S(2)}) async-start(bf16[4,48,1024]{2,1,0:T(8,128)(2,1)} %bitcast.15), calls=%async_computation.3 | async-start | bytes 786432 | tf_op jit(solution)/shard_map/all_to_all | solution.py:98
  16.8 0.1 reshape.84
  17.0 0.1 mul.70
  17.3 0.1 reduce_sum.44
  17.4 0.1 fusion.38
  17.6 0.7 all_to_all.20
  18.4 9.7 %all-to-all-done.3 = bf16[4,48,1024]{2,1,0:T(8,128)(2,1)S(1)} async-done(((bf16[4,48,1024]{2,1,0:T(8,128)(2,1)}), bf16[4,48,1024]{2,1,0:T(8,128)(2,1)S(1)}, u32[]{:S(2)}, u32[]{:S(2)}) %all-to-all-start.3) | async-done | bytes 393248 | tf_op jit(solution)/shard_map/all_to_all | solution.py:98
  28.0 3.2 %all-to-all-start = ((bf16[4,1,48]{2,1,0:T(2,128)(2,1)}), bf16[4,1,48]{2,1,0:T(2,128)(2,1)S(1)}, u32[]{:S(2)}, u32[]{:S(2)}) async-start(bf16[4,1,48]{2,1,0:T(2,128)(2,1)} %all_to_all.20), calls=%async_computation | async-start | bytes 4096 | tf_op jit(solution)/shard_map/all_to_all | solution.py:62
  31.3 1.0 fusion.22
  32.3 4.4 %all-to-all-done = bf16[4,1,48]{2,1,0:T(2,128)(2,1)S(1)} async-done(((bf16[4,1,48]{2,1,0:T(2,128)(2,1)}), bf16[4,1,48]{2,1,0:T(2,128)(2,1)S(1)}, u32[]{:S(2)}, u32[]{:S(2)}) %all-to-all-start) | async-done | bytes 416 | tf_op jit(solution)/shard_map/all_to_all | solution.py:62
  36.7 3.5 %all-to-all-start.1 = ((bf16[4,48,1024]{2,1,0:T(8,128)(2,1)}), bf16[4,48,1024]{2,1,0:T(8,128)(2,1)S(1)}, u32[]{:S(2)}, u32[]{:S(2)}) async-start(bf16[4,48,1024]{2,1,0:T(8,128)(2,1)} %bitcast.4), calls=%async_computation.1 | async-start | bytes 786432 | tf_op jit(solution)/shard_map/all_to_all | solution.py:55
  40.2 10.0 %all-to-all-done.1 = bf16[4,48,1024]{2,1,0:T(8,128)(2,1)S(1)} async-done(((bf16[4,48,1024]{2,1,0:T(8,128)(2,1)}), bf16[4,48,1024]{2,1,0:T(8,128)(2,1)S(1)}, u32[]{:S(2)}, u32[]{:S(2)}) %all-to-all-start.1) | async-done | bytes 393248 | tf_op jit(solution)/shard_map/all_to_all | solution.py:55
  50.2 0.1 multiply_convert_fusion
  50.4 1.4 %fusion.17 = bf16[192,768]{1,0:T(8,128)(2,1)} fusion(bf16[192,1024]{1,0:T(8,128)(2,1)S(1)} %bitcast.75, bf16[1,1,768,1024]{3,2,1,0:T(8,128)(2,1)S(1)} %copy-done), kind=kOutput, calls=%fused_computation.12 | convolution fusion | flops 302137344 | bytes 2260992 | tf_op jit(solution)/shard_map/dot_general | solution.py:74
  51.8 31.7 %all-reduce.2.cloned.1.call-done = bf16[192,768]{1,0:T(8,128)(2,1)} async-done(((bf16[192,768]{1,0:T(8,128)(2,1)}), bf16[192,768]{1,0:T(8,128)(2,1)}) %all-reduce.2.cloned.1.call-update) | async-done | bytes 294928 | tf_op jit(solution)/shard_map/psum | solution.py:82
  83.5 1.4 %fusion.25 = (bf16[192,768]{1,0:T(8,128)(2,1)S(1)}, bf16[192,768]{1,0:T(8,128)(2,1)S(1)}) fusion(bf16[192,768]{1,0:T(8,128)(2,1)} %all-reduce.2.cloned.1.call-done, bf16[1,1,4,48,768]{4,3,2,1,0:T(8,128)(2,1)S(1)} %copy-done.3, bf16[1,1,4,48,768]{4,3,2,1,0:T(8,128)(2,1)} %param.15), kind=kLoop, calls=%fused_computation.24 | loop fusion | flops 2359296 | bytes 1474560 | tf_op jit(solution)/shard_map/convert_element_type | solution.py:34
  84.9 0.7 fusion
  85.5 0.7 copy-done.1
  86.3 1.4 %fusion.11 = bf16[192,1024]{1,0:T(8,128)(2,1)} fusion(f32[192,1024]{1,0:T(8,128)S(1)} %fusion, bf16[192,768]{1,0:T(8,128)(2,1)S(1)} %get-tuple-element.12, bf16[1,1,1024,768]{3,2,1,0:T(8,128)(2,1)S(1)} %copy-done.1), kind=kOutput, calls=%fused_computation.9 | convolution fusion | flops 302383104 | bytes 3047424 | tf_op jit(solution)/shard_map/dot_general | solution.py:87
  87.7 4.6 %all-to-all-start.2 = ((bf16[4,48,1024]{2,1,0:T(8,128)(2,1)}), bf16[4,48,1024]{2,1,0:T(8,128)(2,1)S(1)}, u32[]{:S(2)}, u32[]{:S(2)}) async-start(bf16[4,48,1024]{2,1,0:T(8,128)(2,1)} %bitcast.11), calls=%async_computation.2 | async-start | bytes 786432 | tf_op jit(solution)/shard_map/all_to_all | solution.py:91
  92.3 5.9 %psum.15 = bf16[192]{0:T(256)(128)(2,1)S(1)} all-reduce(bf16[192]{0:T(256)(128)(2,1)S(1)} %get-tuple-element.14), channel_id=1, replica_groups=mesh['section'=2,'dp'=4,'expert'=4] {'dp'}, use_global_device_ids=true, to_apply=%region_6.7 | all-reduce | flops 192 | bytes 768 | tf_op jit(solution)/shard_map/psum | solution.py:105
  98.2 4.7 %all-to-all-done.2 = bf16[4,48,1024]{2,1,0:T(8,128)(2,1)S(1)} async-done(((bf16[4,48,1024]{2,1,0:T(8,128)(2,1)}), bf16[4,48,1024]{2,1,0:T(8,128)(2,1)S(1)}, u32[]{:S(2)}, u32[]{:S(2)}) %all-to-all-start.2) | async-done | bytes 393248 | tf_op jit(solution)/shard_map/all_to_all | solution.py:91
  102.9 0.2 fusion.20
  103.1 1.3 %collective-permute-start = (bf16[64,1024]{1,0:T(8,128)(2,1)S(1)}, bf16[64,1024]{1,0:T(8,128)(2,1)S(1)}, u32[]{:S(2)}, u32[]{:S(2)}) collective-permute-start(bf16[64,1024]{1,0:T(8,128)(2,1)S(1)} %fusion.20), channel_id=1, source_target_pairs={{16,0},{17,1},{18,2},{19,3},{20,4},{21,5},{22,6},{23,7},{24,8},{25... | collective-permute-start | bytes 393224 | tf_op jit(solution)/shard_map/ppermute | solution.py:10
  104.4 0.1 fusion.21
  104.5 0.2 broadcast_in_dim_reshape.4
  104.7 0.6 copy.42
  105.3 4.6 %collective-permute-done = bf16[64,1024]{1,0:T(8,128)(2,1)S(1)} collective-permute-done((bf16[64,1024]{1,0:T(8,128)(2,1)S(1)}, bf16[64,1024]{1,0:T(8,128)(2,1)S(1)}, u32[]{:S(2)}, u32[]{:S(2)}) %collective-permute-start) | collective-permute-done | bytes 131104 | tf_op jit(solution)/shard_map/ppermute | solution.py:10
  109.9 0.7 copy.45
  (32 shorter events, 0.8 us)
Async XLA Ops:
  7.2 1.6 %copy-start = (bf16[1,1,768,1024]{3,2,1,0:T(8,128)(2,1)S(1)}, bf16[1,1,768,1024]{3,2,1,0:T(8,128)(2,1)}, u32[]{:S(2)}) copy-start(bf16[1,1,768,1024]{3,2,1,0:T(8,128)(2,1)} %param.13) | copy-start | bytes 4718596
  8.5 7.8 %copy-start.6 = (s32[1,64,2]{1,2,0:T(2,128)S(1)}, s32[1,64,2]{1,2,0:T(2,128)}, u32[]{:S(2)}) copy-start(s32[1,64,2]{1,2,0:T(2,128)} %param.9) | copy-start | bytes 1540
  8.8 7.9 %copy-start.7 = (bf16[1,64,2]{1,2,0:T(2,128)(2,1)S(1)}, bf16[1,64,2]{1,2,0:T(2,128)(2,1)}, u32[]{:S(2)}) copy-start(bf16[1,64,2]{1,2,0:T(2,128)(2,1)} %param.10) | copy-start | bytes 772
  8.8 22.5 %copy-start.4 = (bf16[1,64,1024]{2,1,0:T(8,128)(2,1)S(1)}, bf16[1,64,1024]{2,1,0:T(8,128)(2,1)}, u32[]{:S(2)}) copy-start(bf16[1,64,1024]{2,1,0:T(8,128)(2,1)} %param.8) | copy-start | bytes 393220
  10.0 18.0 %all-to-all-start.3 = ((bf16[4,48,1024]{2,1,0:T(8,128)(2,1)}), bf16[4,48,1024]{2,1,0:T(8,128)(2,1)S(1)}, u32[]{:S(2)}, u32[]{:S(2)}) async-start(bf16[4,48,1024]{2,1,0:T(8,128)(2,1)} %bitcast.15), calls=%async_computation.3 | async-start | bytes 786432 | tf_op jit(solution)/shard_map/all_to_all | solution.py:98
  28.0 8.7 %all-to-all-start = ((bf16[4,1,48]{2,1,0:T(2,128)(2,1)}), bf16[4,1,48]{2,1,0:T(2,128)(2,1)S(1)}, u32[]{:S(2)}, u32[]{:S(2)}) async-start(bf16[4,1,48]{2,1,0:T(2,128)(2,1)} %all_to_all.20), calls=%async_computation | async-start | bytes 4096 | tf_op jit(solution)/shard_map/all_to_all | solution.py:62
  36.7 13.5 %all-to-all-start.1 = ((bf16[4,48,1024]{2,1,0:T(8,128)(2,1)}), bf16[4,48,1024]{2,1,0:T(8,128)(2,1)S(1)}, u32[]{:S(2)}, u32[]{:S(2)}) async-start(bf16[4,48,1024]{2,1,0:T(8,128)(2,1)} %bitcast.4), calls=%async_computation.1 | async-start | bytes 786432 | tf_op jit(solution)/shard_map/all_to_all | solution.py:55
  40.2 43.3 %all-reduce.2.cloned.1.call-start = ((), (), s32[]{:S(2)}) async-start(), calls=%async_computation.4 | async-start | bytes 589824 | tf_op jit(solution)/shard_map/psum | solution.py:82
  50.2 33.2 %copy-start.3 = (bf16[1,1,4,48,768]{4,3,2,1,0:T(8,128)(2,1)S(1)}, bf16[1,1,4,48,768]{4,3,2,1,0:T(8,128)(2,1)}, u32[]{:S(2)}) copy-start(bf16[1,1,4,48,768]{4,3,2,1,0:T(8,128)(2,1)} %param.14) | copy-start | bytes 884740
  50.4 34.5 %copy-start.2 = (bf16[1,1,1024,768]{3,2,1,0:T(8,128)(2,1)S(1)}, bf16[1,1,1024,768]{3,2,1,0:T(8,128)(2,1)}, u32[]{:S(2)}) copy-start(bf16[1,1,1024,768]{3,2,1,0:T(8,128)(2,1)} %param.12) | copy-start | bytes 4718596
  84.9 1.4 %copy-start.1 = (bf16[1,1,1024,768]{3,2,1,0:T(8,128)(2,1)S(1)}, bf16[1,1,1024,768]{3,2,1,0:T(8,128)(2,1)}, u32[]{:S(2)}) copy-start(bf16[1,1,1024,768]{3,2,1,0:T(8,128)(2,1)} %param.11) | copy-start | bytes 4718596
  86.3 16.6 %copy-start.5 = (bf16[1,64,1024]{2,1,0:T(8,128)(2,1)S(1)}, bf16[1,64,1024]{2,1,0:T(8,128)(2,1)}, u32[]{:S(2)}) copy-start(bf16[1,64,1024]{2,1,0:T(8,128)(2,1)} %param.8) | copy-start | bytes 393220
  87.7 15.2 %all-to-all-start.2 = ((bf16[4,48,1024]{2,1,0:T(8,128)(2,1)}), bf16[4,48,1024]{2,1,0:T(8,128)(2,1)S(1)}, u32[]{:S(2)}, u32[]{:S(2)}) async-start(bf16[4,48,1024]{2,1,0:T(8,128)(2,1)} %bitcast.11), calls=%async_computation.2 | async-start | bytes 786432 | tf_op jit(solution)/shard_map/all_to_all | solution.py:91
  103.1 6.9 %collective-permute-start = (bf16[64,1024]{1,0:T(8,128)(2,1)S(1)}, bf16[64,1024]{1,0:T(8,128)(2,1)S(1)}, u32[]{:S(2)}, u32[]{:S(2)}) collective-permute-start(bf16[64,1024]{1,0:T(8,128)(2,1)S(1)} %fusion.20), channel_id=1, source_target_pairs={{16,0},{17,1},{18,2},{19,3},{20,4},{21,5},{22,6},{23,7},{24,8},{25... | collective-permute-start | bytes 393224 | tf_op jit(solution)/shard_map/ppermute | solution.py:10
Sparse Core Ops, SparseCore 0:
  51.9 31.5 all-reduce.1
where the time goes:
time: 118 us; the launch traced here: 117 us
  waiting for transfers between devices  65.1 us (55%)
  starting transfers between devices  19 us (16%)
  between operations  14.2 us (12%)
  matrix products  6.17 us (5%)
  blocking collectives  5.93 us (5%)
  local copies, waits for them, and re-layouts  4 us (3%)
  other arithmetic  3.1 us (3%)
    psum x1, waiting for transfers between devices, per_device(): lax.psum(hidden_part.astype(jnp.bfloat16), 'dp').astype(jnp.float32)  31.7 us
    all_to_all x1, waiting for transfers between devices, per_device(): lax.all_to_all(send_rows.reshape(experts, capacity, feature_width), 'expe...  10 us
    all_to_all x1, waiting for transfers between devices, per_device(): lax.all_to_all(extra_back, 'expert', split_axis=0, concat_axis=0, tiled=T...  9.65 us
    all_to_all x1, starting transfers between devices, per_device(): lax.all_to_all(extra_back, 'expert', split_axis=0, concat_axis=0, tiled=T...  6.35 us
    psum x1, blocking collectives, per_device(): slot_back = lax.psum(inner_back.astype(jnp.bfloat16), 'dp')  5.93 us
    all_to_all x1, waiting for transfers between devices, per_device(): lax.all_to_all(row_grad.reshape(groups, capacity, feature_width), 'expert...  4.65 us
    ppermute x1, waiting for transfers between devices, shifted(): lax.ppermute(value, axis, [(source, source + steps) for source in range(i...  4.65 us
    all_to_all x1, starting transfers between devices, per_device(): lax.all_to_all(row_grad.reshape(groups, capacity, feature_width), 'expert...  4.6 us
  transfers between devices with their start and end apart: 6, of which 6 were waited for; matrix products, arithmetic and copies ran while one was open for 3% of the time, Pallas kernels for 0%

commit v1 on v0

v1 whole, which is shorter than its diff:
```python
import jax
import jax.numpy as jnp
from jax import lax
from jax.sharding import PartitionSpec as P

AXES = ("section", "dp", "expert")
TRANSPOSED = (((1,), (1,)), ((), ()))


def device_pairs(route):
    sections, parts, experts = (lax.axis_size(name) for name in AXES)
    pairs = []
    for section in range(sections):
        for part in range(parts):
            for expert in range(experts):
                target = route(section, part, expert)
                if target is not None:
                    source_id = (section * parts + part) * experts + expert
                    target_id = (target[0] * parts + target[1]) * experts + target[2]
                    pairs.append((source_id, target_id))
    return pairs


def moved(value, route):
    return lax.ppermute(value, AXES, device_pairs(route))


def matmul(lhs, rhs):
    return jnp.dot(lhs, rhs, preferred_element_type=jnp.float32)


def matmul_t(lhs, rhs):
    return lax.dot_general(lhs, rhs, TRANSPOSED, preferred_element_type=jnp.float32)


def per_device(upstream, routes, gate_weights, w_gate, w_up, w_down, saved_gate, saved_up):
    grads_here = upstream[0]
    route_block = routes[0]
    gates_here = gate_weights[0].astype(jnp.float32)
    parts = lax.axis_size("dp")
    experts = lax.axis_size("expert")
    capacity = saved_gate.shape[3]
    tokens, picks = route_block.shape
    steps = experts // 2
    expert_id = lax.axis_index("expert")
    core = lax.axis_index("dp") & 1

    place = jnp.arange(experts, dtype=jnp.int32)
    labels = expert_id ^ ((place & ~1) + ((place & 1) ^ core))

    named = route_block[:, :, None] == labels[None, None, :]
    names = jnp.any(named, axis=1)
    order = jnp.arange(tokens, dtype=jnp.int32)
    before = (order[None, :] < order[:, None]).astype(jnp.bfloat16)
    earlier = matmul(before, names.astype(jnp.bfloat16)).astype(jnp.int32)
    slot = jnp.where(names, earlier, -1)
    gate_of = jnp.sum(jnp.where(named, gates_here[:, :, None], 0.0), axis=1)
    holds = slot[:, :, None] == jnp.arange(capacity, dtype=jnp.int32)[None, None, :]
    placement = holds.reshape(tokens, experts * capacity).astype(jnp.bfloat16)
    gated = (
        jnp.where(holds, gate_of[:, :, None], 0.0)
        .reshape(tokens, experts * capacity)
        .astype(jnp.bfloat16)
    )
    rows = lax.dot_general(
        placement, grads_here, (((0,), (0,)), ((), ())), preferred_element_type=jnp.float32
    ).astype(jnp.bfloat16)

    def row_block(index):
        return rows[index * capacity : (index + 1) * capacity]

    down_own, gate_own, up_own = (w_down[0, 0], w_gate[0, 0], w_up[0, 0])
    partner = lambda s, d, e: (s, d ^ 1, e)
    down_other = moved(down_own, partner)

    same_core = [moved(row_block(2 * j), lambda s, d, e, j=j: (s, d, e ^ (2 * j + (d & 1)))) for j in range(steps)]
    cross_core = [
        moved(row_block(2 * j + 1), lambda s, d, e, j=j: (s, d ^ 1, e ^ (2 * j + 1 - (d & 1))))
        for j in range(steps)
    ]
    gate_other = moved(gate_own, partner)
    up_other = moved(up_own, partner)

    def expert_back(chosen):
        own = jnp.concatenate([same_core[j] for j in chosen])
        other = jnp.concatenate([cross_core[j] for j in chosen])

        def picked(saved):
            return jnp.concatenate(
                [
                    lax.dynamic_index_in_dim(saved[0, 0], expert_id ^ (2 * j + core), 0, False)
                    for j in chosen
                ]
            ).astype(jnp.float32)

        total = (matmul_t(own, down_own) + matmul_t(other, down_other)).astype(jnp.bfloat16)
        distance = 2
        while distance < parts:
            arrived = moved(total, lambda s, d, e, b=distance: (s, d ^ b, e))
            total = total.astype(jnp.float32) + arrived.astype(jnp.float32)
            distance *= 2
            if distance < parts:
                total = total.astype(jnp.bfloat16)
        total = total.astype(jnp.float32)
        gate_val, up_val = picked(saved_gate), picked(saved_up)
        sigmoid_val = jax.nn.sigmoid(gate_val)
        silu_val = gate_val * sigmoid_val
        hidden = (silu_val * up_val).astype(jnp.bfloat16).astype(jnp.float32)
        slot_grad = jnp.sum(hidden * total, axis=1).astype(jnp.bfloat16)
        gate_back = (
            total * up_val * sigmoid_val * (1.0 + gate_val * (1.0 - sigmoid_val))
        ).astype(jnp.bfloat16)
        up_back = (total * silu_val).astype(jnp.bfloat16)
        row_own = (matmul_t(gate_back, gate_own) + matmul_t(up_back, up_own)).astype(jnp.bfloat16)
        row_other = (matmul_t(gate_back, gate_other) + matmul_t(up_back, up_other)).astype(
            jnp.bfloat16
        )
        return (row_own, row_other, slot_grad)

    near = expert_back([0])
    far = expert_back(list(range(1, steps)))

    def part_of(result, which, j):
        if j == 0:
            return near[which]
        return far[which][(j - 1) * capacity : j * capacity]

    def back_same(j, shift):
        return lambda s, d, e: (s - shift, d, e ^ (2 * j + (d & 1))) if s >= shift else None

    def back_cross(j, shift):
        return lambda s, d, e: (s - shift, d ^ 1, e ^ (2 * j + (d & 1))) if s >= shift else None

    only_later = lambda route: (lambda s, d, e: route(s, d, e) if s >= 1 else None)

    near_rows = jnp.concatenate(
        [
            moved(near[0], only_later(back_same(0, 0))),
            moved(near[1], only_later(back_cross(0, 0))),
        ]
    )
    far_rows = []
    for j in range(1, steps):
        far_rows.append(moved(part_of(far, 0, j), back_same(j, 1)))
        far_rows.append(moved(part_of(far, 1, j), back_cross(j, 1)))
    partial = (
        grads_here.astype(jnp.float32) + matmul(gated[:, : 2 * capacity], near_rows)
    ).astype(jnp.bfloat16)
    message = jnp.concatenate([partial, gated[:, 2 * capacity :]], axis=1)
    message = moved(message, lambda s, d, e: (s - 1, d, e) if s >= 1 else None)
    width = grads_here.shape[1]
    handed = message[:, :width].astype(jnp.float32)
    if far_rows:
        handed = handed + matmul(message[:, width:], jnp.concatenate(far_rows))
    handed = handed.astype(jnp.bfloat16)

    slot_back = []
    for j in range(steps):
        slot_back.append(moved(part_of(None, 2, j)[None], back_same(j, 0)))
        slot_back.append(moved(part_of(None, 2, j)[None], back_cross(j, 0)))
    slot_back = jnp.concatenate(slot_back).astype(jnp.float32)
    back_of = jnp.sum(jnp.where(holds, slot_back[None], 0.0), axis=2)
    gate_grads = jnp.sum(jnp.where(named, back_of[:, None, :], 0.0), axis=2).astype(jnp.bfloat16)
    return (handed[None], gate_grads[None])


def solution(mesh):
    placed = (
        P("section", "expert", "dp"),
        P("section", "expert", None),
        P("section", "expert", None),
        P("section", "expert", "dp", None),
        P("section", "expert", "dp", None),
        P("section", "expert", None, "dp"),
        P("section", "expert", None, None, None),
        P("section", "expert", None, None, None),
    )
    return jax.shard_map(
        per_device,
        mesh=mesh,
        in_specs=placed,
        out_specs=(P("section", "expert", "dp"), P("section", "expert", None)),
        check_vma=False,
    )
```

time: 118 us -> 59.2 us (0.50)
  the two profiles are of different devices: /device:TPU:0 before, /device:TPU:1 now
where the time goes in v1:
time: 59.2 us; the launch traced here: 58.7 us
  starting transfers between devices  22.2 us (38%)
  waiting for transfers between devices  19.5 us (33%)
  matrix products  12.1 us (20%)
  other arithmetic  2.83 us (5%)
  local copies, waits for them, and re-layouts  1.07 us (2%)
  between operations  1.06 us (2%)
    ppermute x18, starting transfers between devices, moved(): return lax.ppermute(value, AXES, device_pairs(route))  22.2 us
    ppermute x18, waiting for transfers between devices, moved(): return lax.ppermute(value, AXES, device_pairs(route))  19.5 us
    dot_general x12, matrix products, matmul_t(): lax.dot_general(lhs, rhs, TRANSPOSED, preferred_element_type=jnp.float32)  9.66 us
    reduce_sum x1, other arithmetic, expert_back(): slot_grad = jnp.sum(hidden * total, axis=1).astype(jnp.bfloat16)  1.29 us
    dot_general x1, matrix products, per_device(): lax.dot_general(placement, grads_here, (((0,), (0,)), ((), ())), preferre...  1.27 us
  transfers between devices with their start and end apart: 18, of which 5 were waited for; matrix products, arithmetic and copies ran while one was open for 26% of the time, Pallas kernels for 0%

profile of v1, /device:TPU:1, one launch (start us, length us, event | category | flops | bytes accessed | tf_op | source)
XLA Modules:
  0.0 58.7 jit_solution(11838488035540792593)
XLA Ops:
  0.7 0.8 %compare_reduce_fusion = pred[64,4]{0,1:T(4,128)(4,1)S(1)} fusion(s32[64,2]{0,1:T(2,128)} %bitcast.87, s32[4]{0:T(128)S(1)} %add_xor_fusion), kind=kLoop, calls=%fused_computation.68 | loop fusion | flops 768 | bytes 784 | tf_op jit(solution)/shard_map/reduce_or | solution.py:52
  1.7 1.3 %convolution_convert_fusion = bf16[192,1024]{1,0:T(8,128)(2,1)S(1)} fusion(pred[64,192]{0,1:T(8,128)(4,1)S(1)} %bitcast.86, bf16[1,64,1024]{2,1,0:T(8,128)(2,1)} %param.8), kind=kOutput, calls=%fused_computation | convolution fusion | flops 25362432 | bytes 536576 | tf_op jit(solution)/shard_map/dot_general | solution.py:65
  3.0 3.7 %collective-permute-start.10 = (bf16[48,1024]{1,0:T(8,128)(2,1)S(1)}, bf16[48,1024]{1,0:T(8,128)(2,1)S(1)}, u32[]{:S(2)}, u32[]{:S(2)}) collective-permute-start(bf16[48,1024]{1,0:T(8,128)(2,1)S(1)} %get-tuple-element.9), channel_id=1, source_target_pairs={{0,7},{1,6},{2,5},{3,4},{4,2},{5,3},{6,0},{7,1},{8,15},{9,14},{10,... | collective-permute-start | bytes 294920 | tf_op jit(solution)/shard_map/ppermute | solution.py:25
  6.7 3.2 %collective-permute-start = (bf16[48,1024]{1,0:T(8,128)(2,1)S(1)}, bf16[48,1024]{1,0:T(8,128)(2,1)S(1)}, u32[]{:S(2)}, u32[]{:S(2)}) collective-permute-start(bf16[48,1024]{1,0:T(8,128)(2,1)S(1)} %get-tuple-element.8), channel_id=1, source_target_pairs={{0,0},{1,1},{2,2},{3,3},{4,5},{5,4},{6,7},{7,6},{8,8},{9,9},{10,10... | collective-permute-start | bytes 294920 | tf_op jit(solution)/shard_map/ppermute | solution.py:25
  10.1 0.9 %collective-permute-done.10 = bf16[48,1024]{1,0:T(8,128)(2,1)S(1)} collective-permute-done((bf16[48,1024]{1,0:T(8,128)(2,1)S(1)}, bf16[48,1024]{1,0:T(8,128)(2,1)S(1)}, u32[]{:S(2)}, u32[]{:S(2)}) %collective-permute-start.10) | collective-permute-done | bytes 98336 | tf_op jit(solution)/shard_map/ppermute | solution.py:25
  11.0 0.9 %collective-permute-start.6 = (bf16[1024,768]{1,0:T(8,128)(2,1)}, bf16[1024,768]{1,0:T(8,128)(2,1)S(1)}, u32[]{:S(2)}, u32[]{:S(2)}) collective-permute-start(bf16[1024,768]{1,0:T(8,128)(2,1)} %bitcast.81), channel_id=1, source_target_pairs={{0,4},{1,5},{2,6},{3,7},{4,0},{5,1},{6,2},{7,3},{8,12},{9,13},{10,... | collective-permute-start | bytes 4718600 | tf_op jit(solution)/shard_map/ppermute | solution.py:25
  11.9 0.6 fusion.55
  12.5 3.7 %collective-permute-done.9 = bf16[48,1024]{1,0:T(8,128)(2,1)S(1)} collective-permute-done((bf16[48,1024]{1,0:T(8,128)(2,1)S(1)}, bf16[48,1024]{1,0:T(8,128)(2,1)S(1)}, u32[]{:S(2)}, u32[]{:S(2)}) %collective-permute-start.9) | collective-permute-done | bytes 98336 | tf_op jit(solution)/shard_map/ppermute | solution.py:25
  16.2 0.6 fusion.6
  16.8 1.3 %collective-permute-start.11 = (bf16[48,768]{1,0:T(8,128)(2,1)S(1)}, bf16[48,768]{1,0:T(8,128)(2,1)S(1)}, u32[]{:S(2)}, u32[]{:S(2)}) collective-permute-start(bf16[48,768]{1,0:T(8,128)(2,1)S(1)} %fusion.6), channel_id=1, source_target_pairs={{0,8},{1,9},{2,10},{3,11},{4,12},{5,13},{6,14},{7,15},{8,0},{9,1},... | collective-permute-start | bytes 221192 | tf_op jit(solution)/shard_map/ppermute | solution.py:25
  18.1 0.6 fusion.54
  18.7 0.6 %fusion.5 = bf16[48,768]{1,0:T(8,128)(2,1)S(1)} fusion(f32[48,768]{1,0:T(8,128)S(1)} %fusion.54, bf16[48,1024]{1,0:T(8,128)(2,1)S(1)} %collective-permute-done, bf16[1,1,768,1024]{3,2,1,0:T(8,128)(2,1)S(1)} %copy-done.2), kind=kOutput, calls=%fused_computation.13 | convolution fusion | flops 75571200 | bytes 1892352 | tf_op jit(solution)/shard_map/dot_general | solution.py:33
  19.7 0.7 %copy.22 = s32[64,192]{1,0:T(8,128)} copy(s32[64,192]{0,1:T(8,128)S(1)} %bitcast.84) | data formatting | bytes 98304 | tf_op jit(solution)/shard_map/eq | solution.py:58
  20.4 2.1 %collective-permute-done.3 = bf16[48,768]{1,0:T(8,128)(2,1)S(1)} collective-permute-done((bf16[48,768]{1,0:T(8,128)(2,1)S(1)}, bf16[48,768]{1,0:T(8,128)(2,1)S(1)}, u32[]{:S(2)}, u32[]{:S(2)}) %collective-permute-start.3) | collective-permute-done | bytes 73760 | tf_op jit(solution)/shard_map/ppermute | solution.py:25
  22.6 1.3 %multiply_reduce_fusion.1 = (bf16[48]{0:T(256)(128)(2,1)S(1)}, bf16[48]{0:T(256)(128)(2,1)S(1)}, bf16[48,768]{1,0:T(8,128)(2,1)S(1)}, bf16[48,768]{1,0:T(8,128)(2,1)S(1)}) fusion(bf16[48,768]{1,0:T(8,128)(2,1)S(1)} %collective-permute-done.3, bf16[48,768]{1,0:T(8,128)(2,1)S(1)} %fusion.5, bf16[1,1,4,48,768]{4,3,2,1,0:T(8,128)(2,1)} %param.15, ...), kind=kLoop, calls=%fused_computation.54 | loop fusion | flops 1548192 | bytes 737480 | tf_op jit(solution)/shard_map/reduce_sum | solution.py:109
  23.8 4.6 %collective-permute-start.17 = (bf16[1,48]{1,0:T(2,128)(2,1)S(1)}, bf16[1,48]{1,0:T(2,128)(2,1)S(1)}, u32[]{:S(2)}, u32[]{:S(2)}) collective-permute-start(bf16[1,48]{1,0:T(2,128)(2,1)S(1)} %bitcast.92), channel_id=1, source_target_pairs={{0,6},{1,7},{2,4},{3,5},{4,3},{5,2},{6,1},{7,0},{8,14},{9,15},{10,... | collective-permute-start | bytes 296 | tf_op jit(solution)/shard_map/ppermute | solution.py:25
  30.3 1.9 %collective-permute-start.14 = (bf16[1,48]{1,0:T(2,128)(2,1)S(1)}, bf16[1,48]{1,0:T(2,128)(2,1)S(1)}, u32[]{:S(2)}, u32[]{:S(2)}) collective-permute-start(bf16[1,48]{1,0:T(2,128)(2,1)S(1)} %bitcast.91), channel_id=1, source_target_pairs={{0,0},{1,1},{2,2},{3,3},{4,5},{5,4},{6,7},{7,6},{8,8},{9,9},{10,10... | collective-permute-start | bytes 296 | tf_op jit(solution)/shard_map/ppermute | solution.py:25
  32.2 0.6 fusion.51
  32.8 0.6 fusion.1
  33.4 0.6 fusion.3
  34.0 0.8 %collective-permute-start.4 = (bf16[48,1024]{1,0:T(8,128)(2,1)S(1)}, bf16[48,1024]{1,0:T(8,128)(2,1)S(1)}, u32[]{:S(2)}, u32[]{:S(2)}) collective-permute-start(bf16[48,1024]{1,0:T(8,128)(2,1)S(1)} %fusion.1), channel_id=1, source_target_pairs={{16,16},{17,17},{18,18},{19,19},{20,21},{21,20},{22,23},{23,22},{2... | collective-permute-start | bytes 294920 | tf_op jit(solution)/shard_map/ppermute | solution.py:25
  34.8 2.0 %fusion.2 = bf16[48,1024]{1,0:T(8,128)(2,1)S(1)} fusion(f32[48,1024]{1,0:T(8,128)S(1)} %fusion.51, bf16[48,768]{1,0:T(8,128)(2,1)S(1)} %get-tuple-element.6, bf16[1024,768]{1,0:T(8,128)(2,1)} %collective-permute-done.5), kind=kOutput, calls=%fused_computation.8 | convolution fusion | flops 75595776 | bytes 1941504 | tf_op jit(solution)/shard_map/dot_general | solution.py:33
  36.8 0.6 fusion.52
  37.4 1.3 %collective-permute-start.12 = (bf16[48,1024]{1,0:T(8,128)(2,1)S(1)}, bf16[48,1024]{1,0:T(8,128)(2,1)S(1)}, u32[]{:S(2)}, u32[]{:S(2)}) collective-permute-start(bf16[48,1024]{1,0:T(8,128)(2,1)S(1)} %fusion.3), channel_id=1, source_target_pairs={{16,2},{17,3},{18,0},{19,1},{20,7},{21,6},{22,5},{23,4},{24,10},{2... | collective-permute-start | bytes 294920 | tf_op jit(solution)/shard_map/ppermute | solution.py:25
  38.7 0.7 %collective-permute-start.7 = (bf16[48,1024]{1,0:T(8,128)(2,1)S(1)}, bf16[48,1024]{1,0:T(8,128)(2,1)S(1)}, u32[]{:S(2)}, u32[]{:S(2)}) collective-permute-start(bf16[48,1024]{1,0:T(8,128)(2,1)S(1)} %fusion.2), channel_id=1, source_target_pairs={{16,20},{17,21},{18,22},{19,23},{20,17},{21,16},{22,19},{23,18},{2... | collective-permute-start | bytes 294920 | tf_op jit(solution)/shard_map/ppermute | solution.py:25
  39.6 0.6 %fusion.40 = (bf16[64,2]{0,1:T(2,128)(2,1)}, bf16[64,4]{0,1:T(4,128)(2,1)S(1)}) fusion(f32[64,4]{0,1:T(4,128)S(1)} %select_reduce_fusion, s32[64,2]{0,1:T(2,128)S(1)} %bitcast.88, s32[4]{0:T(128)S(1)} %add_xor_fusion, f32[64,2]{0,1:T(2,128)S(1)} %bitcast_convert_fusion), kind=kLoop, calls=%fused_computation.70 | loop fusion | flops 2176 | bytes 2832 | tf_op jit(solution)/shard_map/reduce_sum | solution.py:163
  40.6 1.3 %collective-permute-start.8 = (bf16[64,1120]{1,0:T(8,128)(2,1)S(1)}, bf16[64,1120]{1,0:T(8,128)(2,1)S(1)}, u32[]{:S(2)}, u32[]{:S(2)}) collective-permute-start(bf16[64,1120]{1,0:T(8,128)(2,1)S(1)} %pad_maximum_fusion), channel_id=1, source_target_pairs={{16,0},{17,1},{18,2},{19,3},{20,4},{21,5},{22,6},{23,7},{24,8},{25... | collective-permute-start | bytes 430088 | tf_op jit(solution)/shard_map/ppermute | solution.py:25
  41.9 2.0 %fusion.4 = bf16[48,1024]{1,0:T(8,128)(2,1)S(1)} fusion(f32[48,1024]{1,0:T(8,128)S(1)} %fusion.52, bf16[48,768]{1,0:T(8,128)(2,1)S(1)} %get-tuple-element.7, bf16[1024,768]{1,0:T(8,128)(2,1)} %collective-permute-done.5), kind=kOutput, calls=%fused_computation.10 | convolution fusion | flops 75595776 | bytes 1941504 | tf_op jit(solution)/shard_map/dot_general | solution.py:33
  43.9 1.3 %collective-permute-start.13 = (bf16[48,1024]{1,0:T(8,128)(2,1)S(1)}, bf16[48,1024]{1,0:T(8,128)(2,1)S(1)}, u32[]{:S(2)}, u32[]{:S(2)}) collective-permute-start(bf16[48,1024]{1,0:T(8,128)(2,1)S(1)} %fusion.4), channel_id=1, source_target_pairs={{16,6},{17,7},{18,4},{19,5},{20,3},{21,2},{22,1},{23,0},{24,14},{2... | collective-permute-start | bytes 294920 | tf_op jit(solution)/shard_map/ppermute | solution.py:25
  45.2 2.0 %collective-permute-done.12 = bf16[48,1024]{1,0:T(8,128)(2,1)S(1)} collective-permute-done((bf16[48,1024]{1,0:T(8,128)(2,1)S(1)}, bf16[48,1024]{1,0:T(8,128)(2,1)S(1)}, u32[]{:S(2)}, u32[]{:S(2)}) %collective-permute-start.12) | collective-permute-done | bytes 98336 | tf_op jit(solution)/shard_map/ppermute | solution.py:25
  47.2 10.7 %collective-permute-done.13 = bf16[48,1024]{1,0:T(8,128)(2,1)S(1)} collective-permute-done((bf16[48,1024]{1,0:T(8,128)(2,1)S(1)}, bf16[48,1024]{1,0:T(8,128)(2,1)S(1)}, u32[]{:S(2)}, u32[]{:S(2)}) %collective-permute-start.13) | collective-permute-done | bytes 98336 | tf_op jit(solution)/shard_map/ppermute | solution.py:25
  57.9 0.8 %fusion.15 = bf16[1,64,1024]{2,1,0:T(8,128)(2,1)} fusion(bf16[48,1024]{1,0:T(8,128)(2,1)S(1)} %collective-permute-done.13, bf16[48,1024]{1,0:T(8,128)(2,1)S(1)} %collective-permute-done.12, bf16[64,1120]{1,0:T(8,128)(2,1)S(1)} %collective-permute-done.8), kind=kOutput, calls=%fused_computation.29 | convolution fusion | flops 13172736 | bytes 471040 | tf_op jit(solution)/shard_map/dot_general | solution.py:29
  (54 shorter events, 3.2 us)
Async XLA Ops:
  0.6 11.3 %collective-permute-start.2 = (bf16[768,1024]{1,0:T(8,128)(2,1)}, bf16[768,1024]{1,0:T(8,128)(2,1)S(1)}, u32[]{:S(2)}, u32[]{:S(2)}) collective-permute-start(bf16[768,1024]{1,0:T(8,128)(2,1)} %bitcast.83), channel_id=1, source_target_pairs={{0,4},{1,5},{2,6},{3,7},{4,0},{5,1},{6,2},{7,3},{8,12},{9,13},{10,... | collective-permute-start | bytes 4718600 | tf_op jit(solution)/shard_map/ppermute | solution.py:25
  1.7 14.5 %copy-start.2 = (bf16[1,1,768,1024]{3,2,1,0:T(8,128)(2,1)S(1)}, bf16[1,1,768,1024]{3,2,1,0:T(8,128)(2,1)}, u32[]{:S(2)}) copy-start(bf16[1,1,768,1024]{3,2,1,0:T(8,128)(2,1)} %param.13) | copy-start | bytes 4718596
  3.0 8.0 %collective-permute-start.10 = (bf16[48,1024]{1,0:T(8,128)(2,1)S(1)}, bf16[48,1024]{1,0:T(8,128)(2,1)S(1)}, u32[]{:S(2)}, u32[]{:S(2)}) collective-permute-start(bf16[48,1024]{1,0:T(8,128)(2,1)S(1)} %get-tuple-element.9), channel_id=1, source_target_pairs={{0,7},{1,6},{2,5},{3,4},{4,2},{5,3},{6,0},{7,1},{8,15},{9,14},{10,... | collective-permute-start | bytes 294920 | tf_op jit(solution)/shard_map/ppermute | solution.py:25
  6.7 12.0 %collective-permute-start = (bf16[48,1024]{1,0:T(8,128)(2,1)S(1)}, bf16[48,1024]{1,0:T(8,128)(2,1)S(1)}, u32[]{:S(2)}, u32[]{:S(2)}) collective-permute-start(bf16[48,1024]{1,0:T(8,128)(2,1)S(1)} %get-tuple-element.8), channel_id=1, source_target_pairs={{0,0},{1,1},{2,2},{3,3},{4,5},{5,4},{6,7},{7,6},{8,8},{9,9},{10,10... | collective-permute-start | bytes 294920 | tf_op jit(solution)/shard_map/ppermute | solution.py:25
  9.9 6.3 %collective-permute-start.9 = (bf16[48,1024]{1,0:T(8,128)(2,1)S(1)}, bf16[48,1024]{1,0:T(8,128)(2,1)S(1)}, u32[]{:S(2)}, u32[]{:S(2)}) collective-permute-start(bf16[48,1024]{1,0:T(8,128)(2,1)S(1)} %get-tuple-element.10), channel_id=1, source_target_pairs={{0,2},{1,3},{2,0},{3,1},{4,7},{5,6},{6,5},{7,4},{8,10},{9,11},{10,... | collective-permute-start | bytes 294920 | tf_op jit(solution)/shard_map/ppermute | solution.py:25
  10.0 8.1 %collective-permute-start.1 = (bf16[48,1024]{1,0:T(8,128)(2,1)S(1)}, bf16[48,1024]{1,0:T(8,128)(2,1)S(1)}, u32[]{:S(2)}, u32[]{:S(2)}) collective-permute-start(bf16[48,1024]{1,0:T(8,128)(2,1)S(1)} %get-tuple-element.11), channel_id=1, source_target_pairs={{0,5},{1,4},{2,7},{3,6},{4,0},{5,1},{6,2},{7,3},{8,13},{9,12},{10,... | collective-permute-start | bytes 294920 | tf_op jit(solution)/shard_map/ppermute | solution.py:25
  11.0 19.3 %collective-permute-start.6 = (bf16[1024,768]{1,0:T(8,128)(2,1)}, bf16[1024,768]{1,0:T(8,128)(2,1)S(1)}, u32[]{:S(2)}, u32[]{:S(2)}) collective-permute-start(bf16[1024,768]{1,0:T(8,128)(2,1)} %bitcast.81), channel_id=1, source_target_pairs={{0,4},{1,5},{2,6},{3,7},{4,0},{5,1},{6,2},{7,3},{8,12},{9,13},{10,... | collective-permute-start | bytes 4718600 | tf_op jit(solution)/shard_map/ppermute | solution.py:25
  11.9 22.1 %collective-permute-start.5 = (bf16[1024,768]{1,0:T(8,128)(2,1)}, bf16[1024,768]{1,0:T(8,128)(2,1)}, u32[]{:S(2)}, u32[]{:S(2)}) collective-permute-start(bf16[1024,768]{1,0:T(8,128)(2,1)} %bitcast.82), channel_id=1, source_target_pairs={{0,4},{1,5},{2,6},{3,7},{4,0},{5,1},{6,2},{7,3},{8,12},{9,13},{10,... | collective-permute-start | bytes 4718600 | tf_op jit(solution)/shard_map/ppermute | solution.py:25
  16.8 2.8 %copy-start.7 = (bf16[1,64,2]{1,2,0:T(2,128)(2,1)S(1)}, bf16[1,64,2]{1,2,0:T(2,128)(2,1)}, u32[]{:S(2)}) copy-start(bf16[1,64,2]{1,2,0:T(2,128)(2,1)} %param.10) | copy-start | bytes 772
  16.8 3.6 %collective-permute-start.11 = (bf16[48,768]{1,0:T(8,128)(2,1)S(1)}, bf16[48,768]{1,0:T(8,128)(2,1)S(1)}, u32[]{:S(2)}, u32[]{:S(2)}) collective-permute-start(bf16[48,768]{1,0:T(8,128)(2,1)S(1)} %fusion.6), channel_id=1, source_target_pairs={{0,8},{1,9},{2,10},{3,11},{4,12},{5,13},{6,14},{7,15},{8,0},{9,1},... | collective-permute-start | bytes 221192 | tf_op jit(solution)/shard_map/ppermute | solution.py:25
  18.7 10.5 %copy-start.1 = (bf16[1,1,1024,768]{3,2,1,0:T(8,128)(2,1)S(1)}, bf16[1,1,1024,768]{3,2,1,0:T(8,128)(2,1)}, u32[]{:S(2)}) copy-start(bf16[1,1,1024,768]{3,2,1,0:T(8,128)(2,1)} %param.11) | copy-start | bytes 4718596
  19.3 3.3 %collective-permute-start.3 = (bf16[48,768]{1,0:T(8,128)(2,1)S(1)}, bf16[48,768]{1,0:T(8,128)(2,1)S(1)}, u32[]{:S(2)}, u32[]{:S(2)}) collective-permute-start(bf16[48,768]{1,0:T(8,128)(2,1)S(1)} %fusion.5), channel_id=1, source_target_pairs={{0,8},{1,9},{2,10},{3,11},{4,12},{5,13},{6,14},{7,15},{8,0},{9,1},... | collective-permute-start | bytes 221192 | tf_op jit(solution)/shard_map/ppermute | solution.py:25
  23.8 13.6 %collective-permute-start.17 = (bf16[1,48]{1,0:T(2,128)(2,1)S(1)}, bf16[1,48]{1,0:T(2,128)(2,1)S(1)}, u32[]{:S(2)}, u32[]{:S(2)}) collective-permute-start(bf16[1,48]{1,0:T(2,128)(2,1)S(1)} %bitcast.92), channel_id=1, source_target_pairs={{0,6},{1,7},{2,4},{3,5},{4,3},{5,2},{6,1},{7,0},{8,14},{9,15},{10,... | collective-permute-start | bytes 296 | tf_op jit(solution)/shard_map/ppermute | solution.py:25
  28.5 10.2 %collective-permute-start.16 = (bf16[1,48]{1,0:T(2,128)(2,1)S(1)}, bf16[1,48]{1,0:T(2,128)(2,1)S(1)}, u32[]{:S(2)}, u32[]{:S(2)}) collective-permute-start(bf16[1,48]{1,0:T(2,128)(2,1)S(1)} %bitcast.93), channel_id=1, source_target_pairs={{0,2},{1,3},{2,0},{3,1},{4,7},{5,6},{6,5},{7,4},{8,10},{9,11},{10,... | collective-permute-start | bytes 296 | tf_op jit(solution)/shard_map/ppermute | solution.py:25
  29.0 10.4 %collective-permute-start.15 = (bf16[1,48]{1,0:T(2,128)(2,1)S(1)}, bf16[1,48]{1,0:T(2,128)(2,1)S(1)}, u32[]{:S(2)}, u32[]{:S(2)}) collective-permute-start(bf16[1,48]{1,0:T(2,128)(2,1)S(1)} %bitcast.90), channel_id=1, source_target_pairs={{0,4},{1,5},{2,6},{3,7},{4,1},{5,0},{6,3},{7,2},{8,12},{9,13},{10,... | collective-permute-start | bytes 296 | tf_op jit(solution)/shard_map/ppermute | solution.py:25
  29.1 3.1 %copy-start.3 = (bf16[1,1,4,48,768]{4,3,2,1,0:T(8,128)(2,1)S(1)}, bf16[1,1,4,48,768]{4,3,2,1,0:T(8,128)(2,1)}, u32[]{:S(2)}) copy-start(bf16[1,1,4,48,768]{4,3,2,1,0:T(8,128)(2,1)} %param.14) | copy-start | bytes 884740
  29.7 3.1 %copy-start = (bf16[1,1,1024,768]{3,2,1,0:T(8,128)(2,1)S(1)}, bf16[1,1,1024,768]{3,2,1,0:T(8,128)(2,1)}, u32[]{:S(2)}) copy-start(bf16[1,1,1024,768]{3,2,1,0:T(8,128)(2,1)} %param.12) | copy-start | bytes 4718596
  30.3 9.1 %collective-permute-start.14 = (bf16[1,48]{1,0:T(2,128)(2,1)S(1)}, bf16[1,48]{1,0:T(2,128)(2,1)S(1)}, u32[]{:S(2)}, u32[]{:S(2)}) collective-permute-start(bf16[1,48]{1,0:T(2,128)(2,1)S(1)} %bitcast.91), channel_id=1, source_target_pairs={{0,0},{1,1},{2,2},{3,3},{4,5},{5,4},{6,7},{7,6},{8,8},{9,9},{10,10... | collective-permute-start | bytes 296 | tf_op jit(solution)/shard_map/ppermute | solution.py:25
  34.0 5.6 %copy-start.6 = (s32[1,64,2]{1,2,0:T(2,128)S(1)}, s32[1,64,2]{1,2,0:T(2,128)}, u32[]{:S(2)}) copy-start(s32[1,64,2]{1,2,0:T(2,128)} %param.9) | copy-start | bytes 1540
  34.0 6.3 %copy-start.5 = (s32[64,192]{1,0:T(8,128)S(1)}, s32[64,192]{1,0:T(8,128)}, u32[]{:S(2)}) copy-start(s32[64,192]{1,0:T(8,128)} %copy.22) | copy-start | bytes 147460
  34.0 6.3 %collective-permute-start.4 = (bf16[48,1024]{1,0:T(8,128)(2,1)S(1)}, bf16[48,1024]{1,0:T(8,128)(2,1)S(1)}, u32[]{:S(2)}, u32[]{:S(2)}) collective-permute-start(bf16[48,1024]{1,0:T(8,128)(2,1)S(1)} %fusion.1), channel_id=1, source_target_pairs={{16,16},{17,17},{18,18},{19,19},{20,21},{21,20},{22,23},{23,22},{2... | collective-permute-start | bytes 294920 | tf_op jit(solution)/shard_map/ppermute | solution.py:25
  36.8 3.6 %copy-start.4 = (bf16[1,64,1024]{2,1,0:T(8,128)(2,1)S(1)}, bf16[1,64,1024]{2,1,0:T(8,128)(2,1)}, u32[]{:S(2)}) copy-start(bf16[1,64,1024]{2,1,0:T(8,128)(2,1)} %param.8) | copy-start | bytes 393220
  37.4 9.7 %collective-permute-start.12 = (bf16[48,1024]{1,0:T(8,128)(2,1)S(1)}, bf16[48,1024]{1,0:T(8,128)(2,1)S(1)}, u32[]{:S(2)}, u32[]{:S(2)}) collective-permute-start(bf16[48,1024]{1,0:T(8,128)(2,1)S(1)} %fusion.3), channel_id=1, source_target_pairs={{16,2},{17,3},{18,0},{19,1},{20,7},{21,6},{22,5},{23,4},{24,10},{2... | collective-permute-start | bytes 294920 | tf_op jit(solution)/shard_map/ppermute | solution.py:25
  38.7 1.6 %collective-permute-start.7 = (bf16[48,1024]{1,0:T(8,128)(2,1)S(1)}, bf16[48,1024]{1,0:T(8,128)(2,1)S(1)}, u32[]{:S(2)}, u32[]{:S(2)}) collective-permute-start(bf16[48,1024]{1,0:T(8,128)(2,1)S(1)} %fusion.2), channel_id=1, source_target_pairs={{16,20},{17,21},{18,22},{19,23},{20,17},{21,16},{22,19},{23,18},{2... | collective-permute-start | bytes 294920 | tf_op jit(solution)/shard_map/ppermute | solution.py:25
  40.6 17.3 %collective-permute-start.8 = (bf16[64,1120]{1,0:T(8,128)(2,1)S(1)}, bf16[64,1120]{1,0:T(8,128)(2,1)S(1)}, u32[]{:S(2)}, u32[]{:S(2)}) collective-permute-start(bf16[64,1120]{1,0:T(8,128)(2,1)S(1)} %pad_maximum_fusion), channel_id=1, source_target_pairs={{16,0},{17,1},{18,2},{19,3},{20,4},{21,5},{22,6},{23,7},{24,8},{25... | collective-permute-start | bytes 430088 | tf_op jit(solution)/shard_map/ppermute | solution.py:25
  43.9 14.0 %collective-permute-start.13 = (bf16[48,1024]{1,0:T(8,128)(2,1)S(1)}, bf16[48,1024]{1,0:T(8,128)(2,1)S(1)}, u32[]{:S(2)}, u32[]{:S(2)}) collective-permute-start(bf16[48,1024]{1,0:T(8,128)(2,1)S(1)} %fusion.4), channel_id=1, source_target_pairs={{16,6},{17,7},{18,4},{19,5},{20,3},{21,2},{22,1},{23,0},{24,14},{2... | collective-permute-start | bytes 294920 | tf_op jit(solution)/shard_map/ppermute | solution.py:25

commit v2 on v1

v2 whole, which is shorter than its diff:
```python
import functools

import jax
import jax.numpy as jnp
from jax import lax
from jax.experimental import pallas as pl
from jax.experimental.pallas import tpu as pltpu
from jax.sharding import PartitionSpec as P


AXES = ("section", "dp", "expert")
TRANSPOSED = (((1,), (1,)), ((), ()))
LEADING = (((0,), (0,)), ((), ()))


def device_pairs(route):
    sections, parts, experts = (lax.axis_size(name) for name in AXES)
    pairs = []
    for section in range(sections):
        for part in range(parts):
            for expert in range(experts):
                target = route(section, part, expert)
                if target is not None:
                    source_id = (section * parts + part) * experts + expert
                    target_id = (target[0] * parts + target[1]) * experts + target[2]
                    pairs.append((source_id, target_id))
    return pairs


def moved(value, route):
    return lax.ppermute(value, AXES, device_pairs(route))


def matmul(lhs, rhs):
    return jnp.dot(lhs, rhs, preferred_element_type=jnp.float32)


def matmul_t(lhs, rhs):
    return lax.dot_general(lhs, rhs, TRANSPOSED, preferred_element_type=jnp.float32)


def kernel_call(body, outs, ins, flops=0, spaces=None, scratch=()):
    spaces = spaces or [pltpu.VMEM] * len(ins)
    ins = [
        pltpu.with_memory_space_constraint(value, space) if space == pltpu.HBM else value
        for value, space in zip(ins, spaces)
    ]
    size = sum(value.size * value.dtype.itemsize for value in ins)
    return pl.pallas_call(
        body,
        out_shape=outs,
        in_specs=[pl.BlockSpec(memory_space=space) for space in spaces],
        out_specs=jax.tree.map(lambda _: pl.BlockSpec(memory_space=pltpu.VMEM), outs),
        scratch_shapes=scratch,
        compiler_params=pltpu.CompilerParams(vmem_limit_bytes=16 * 2**20),
        cost_estimate=pl.CostEstimate(flops=flops, bytes_accessed=size, transcendentals=0),
    )(*ins)


def table_kernel(capacity, experts, expert_ref, route_hbm, gate_hbm, grads_hbm, *refs):
    row_refs, (gated_ref, hold_ref) = (refs[:experts], refs[experts : experts + 2])
    route_ref, gate_ref, grads_ref, semaphores = refs[experts + 2 :]
    copies = [
        pltpu.make_async_copy(source, target, semaphores.at[index])
        for index, (source, target) in enumerate(
            ((route_hbm, route_ref), (gate_hbm, gate_ref), (grads_hbm, grads_ref))
        )
    ]
    for copy in copies:
        copy.start()
    picks, tokens = route_ref.shape
    slots = experts * capacity
    place = lax.broadcasted_iota(jnp.int32, (slots, 1), 0)
    block = lax.div(place, capacity)
    inside = (place - block * capacity).astype(jnp.float32)
    label = expert_ref[0] ^ block
    row = lax.broadcasted_iota(jnp.int32, (tokens, tokens), 0)
    column = lax.broadcasted_iota(jnp.int32, (tokens, tokens), 1)
    before = jnp.where(row < column, 1.0, 0.0).astype(jnp.bfloat16)
    copies[0].wait()
    named = [route_ref[pick : pick + 1, :] == label for pick in range(picks)]
    names = functools.reduce(jnp.logical_or, named)
    earlier = matmul(jnp.where(names, 1.0, 0.0).astype(jnp.bfloat16), before)
    fits = earlier == inside
    placed = jnp.where(names & fits, 1.0, 0.0).astype(jnp.bfloat16)
    copies[2].wait()
    for k, ref in enumerate(row_refs):
        ref[...] = matmul(placed[k * capacity : (k + 1) * capacity], grads_ref[...]).astype(
            jnp.bfloat16
        )
    copies[1].wait()
    gated = jnp.zeros((slots, tokens), jnp.float32)
    for pick in range(picks):
        here = jnp.where(named[pick] & fits, 1.0, 0.0)
        hold_ref[pick] = here.astype(jnp.bfloat16)
        gated = gated + here * gate_ref[pick : pick + 1, :].astype(jnp.float32)
    gated_ref[...] = gated.astype(jnp.bfloat16)


def fetch_kernel(*refs):
    count = len(refs) // 2
    copies = [
        pltpu.make_async_copy(refs[index], refs[count + index], refs[-1].at[index])
        for index in range(count)
    ]
    for copy in copies:
        copy.start()
    for copy in copies:
        copy.wait()


def raw_kernel(*refs):
    row_refs, down_ref, out_ref = (refs[:-2], refs[-2], refs[-1])
    rows = jnp.concatenate([ref[...] for ref in row_refs])
    out_ref[...] = matmul_t(rows, down_ref[...]).astype(jnp.bfloat16)


def back_kernel(offsets, capacity, near, expert_ref, here_ref, other_ref, saved_gate_ref, saved_up_ref, gate_ref, up_ref, *refs):
    total = here_ref[...].astype(jnp.float32) + other_ref[...].astype(jnp.float32)

    def picked(ref):
        return jnp.concatenate([ref[expert_ref[0] ^ k] for k in offsets]).astype(jnp.float32)

    gate_val, up_val = (picked(saved_gate_ref), picked(saved_up_ref))
    sigmoid_val = jax.nn.sigmoid(gate_val)
    silu_val = gate_val * sigmoid_val
    hidden = (silu_val * up_val).astype(jnp.bfloat16).astype(jnp.float32)
    inner = jnp.sum(hidden * total, axis=1, keepdims=True)
    gate_back = (
        total * up_val * sigmoid_val * (1.0 + gate_val * (1.0 - sigmoid_val))
    ).astype(jnp.bfloat16)
    up_back = (total * silu_val).astype(jnp.bfloat16)
    back = (matmul_t(gate_back, gate_ref[...]) + matmul_t(up_back, up_ref[...])).astype(
        jnp.bfloat16
    )
    inner = jnp.broadcast_to(inner, (inner.shape[0], 128)).astype(jnp.bfloat16)
    outs = iter(refs)
    for index, k in enumerate(offsets):
        own = slice(index * capacity, (index + 1) * capacity)
        if near and k:
            joined = next(outs)
            joined[:, : back.shape[1]] = back[own]
            joined[:, back.shape[1] :] = inner[own]
        else:
            next(outs)[...] = back[own]
            next(outs)[...] = inner[own]


def partial_kernel(grads_ref, gated_ref, first_ref, *refs):
    row_refs, message_ref = (refs[:-1], refs[-1])
    tokens, width = grads_ref.shape
    rows = jnp.concatenate([first_ref[...]] + [ref[:, :width] for ref in row_refs])
    near = rows.shape[0]
    partial = grads_ref[...].astype(jnp.float32) + lax.dot_general(
        gated_ref[:near], rows, LEADING, preferred_element_type=jnp.float32
    )
    message_ref[:, :width] = partial.astype(jnp.bfloat16)
    row = lax.broadcasted_iota(jnp.int32, (tokens, tokens), 0)
    column = lax.broadcasted_iota(jnp.int32, (tokens, tokens), 1)
    same = jnp.where(row == column, 1.0, 0.0).astype(jnp.bfloat16)
    message_ref[:, width:] = matmul_t(same, gated_ref[near:]).astype(jnp.bfloat16)


def combine_kernel(message_ref, *refs):
    row_refs, out_ref = (refs[:-1], refs[-1])
    width = out_ref.shape[1]
    rows = jnp.concatenate([ref[...] for ref in row_refs])
    gated = message_ref[:, width:]
    out_ref[...] = (
        message_ref[:, :width].astype(jnp.float32) + matmul(gated, rows)
    ).astype(jnp.bfloat16)


def gates_kernel(hold_ref, *refs):
    slot_refs, out_ref = (refs[:-1], refs[-1])
    slots = jnp.concatenate([ref[:, ref.shape[1] - 128 :] for ref in slot_refs])
    for pick in range(hold_ref.shape[0]):
        found = lax.dot_general(
            slots, hold_ref[pick], LEADING, preferred_element_type=jnp.float32
        )
        out_ref[pick : pick + 1, :] = found[:1].astype(jnp.bfloat16)


def layer(upstream, routes, gate_weights, w_gate, w_up, w_down, saved_gate, saved_up):
    grads_here = upstream[0]
    route_block = routes[0]
    parts = lax.axis_size("dp")
    experts = lax.axis_size("expert")
    capacity = saved_gate.shape[3]
    tokens, picks = route_block.shape
    width = grads_here.shape[1]
    units = w_down.shape[2]
    expert_id = lax.axis_index("expert").astype(jnp.int32)[None]
    bf16 = lambda *shape: jax.ShapeDtypeStruct(shape, jnp.bfloat16)

    *rows, gated, holds = kernel_call(
        functools.partial(table_kernel, capacity, experts),
        (
            *[bf16(capacity, width)] * experts,
            bf16(experts * capacity, tokens),
            bf16(picks, experts * capacity, tokens),
        ),
        (expert_id, route_block.T, gate_weights[0].T, grads_here),
        2 * experts * capacity * tokens * width,
        [pltpu.SMEM] + [pltpu.HBM] * 3,
        (
            pltpu.VMEM((picks, tokens), jnp.int32),
            pltpu.VMEM((picks, tokens), jnp.bfloat16),
            pltpu.VMEM((tokens, width), jnp.bfloat16),
            pltpu.SemaphoreType.DMA((3,)),
        ),
    )

    def across(k, shift=0):
        return lambda s, d, e: (s - shift, d, e ^ k) if s >= shift else None

    half = experts // 2
    far = [k for k in range(half, experts)]
    cut = (len(far) + 1) // 2
    chunks = {"a": far[:cut], "b": far[cut:], "c": list(range(half))}
    arrived = {0: rows[0]}
    for name in ("a", "b", "c"):
        for k in chunks[name]:
            if k:
                arrived[k] = moved(rows[k], across(k))

    held = (w_down[0, 0], w_gate[0, 0], w_up[0, 0], saved_gate[0, 0], saved_up[0, 0])
    down, gate, up, gate_pre, up_pre = kernel_call(
        fetch_kernel,
        tuple(bf16(*value.shape) for value in held),
        held,
        0,
        [pltpu.HBM] * len(held),
        (pltpu.SemaphoreType.DMA((len(held),)),),
    )
    row_grad, slot_grad = ({}, {})
    for name in ("a", "b", "c"):
        chosen = chunks[name]
        count = len(chosen) * capacity
        total = kernel_call(
            raw_kernel,
            bf16(count, units),
            (*[arrived[k] for k in chosen], down),
            2 * count * width * units,
        )
        distance = 1
        while distance < parts:
            other = moved(total, lambda s, d, e, b=distance: (s, d ^ b, e))
            distance *= 2
            if distance < parts:
                total = (total.astype(jnp.float32) + other.astype(jnp.float32)).astype(jnp.bfloat16)
        near = name == "c"
        outs = []
        for k in chosen:
            if near and k:
                outs.append(bf16(capacity, width + 128))
            else:
                outs.extend([bf16(capacity, width), bf16(capacity, 128)])
        results = list(
            kernel_call(
                functools.partial(back_kernel, tuple(chosen), capacity, near),
                tuple(outs),
                (expert_id, total, other, gate_pre, up_pre, gate, up),
                4 * count * width * units,
                [pltpu.SMEM] + [pltpu.VMEM] * 6,
            )
        )
        for k in chosen:
            row_grad[k] = results.pop(0)
            if not (near and k):
                slot_grad[k] = results.pop(0)

    returned = {}
    for name in ("a", "b", "c"):
        for k in chunks[name]:
            if k:
                returned[k] = moved(row_grad[k], across(k, 0 if name == "c" else 1))
    message = kernel_call(
        partial_kernel,
        bf16(tokens, width + half * capacity),
        (grads_here, gated, row_grad[0], *[returned[k] for k in range(1, half)]),
        2 * tokens * width * half * capacity,
    )
    message = moved(message, lambda s, d, e: (s - 1, d, e) if s >= 1 else None)
    handed = kernel_call(
        combine_kernel,
        bf16(tokens, width),
        (message, *[returned[k] for k in far]),
        2 * tokens * width * half * capacity,
    )
    slot_back = [slot_grad[0], *[returned[k] for k in range(1, half)]]
    for k in far:
        slot_back.append(moved(slot_grad[k], across(k)))
    gate_grads = kernel_call(gates_kernel, bf16(picks, tokens), (holds, *slot_back))
    return (handed[None], gate_grads.T[None])


def solution(mesh):
    placed = (
        P("section", "expert", "dp"),
        P("section", "expert", None),
        P("section", "expert", None),
        P("section", "expert", "dp", None),
        P("section", "expert", "dp", None),
        P("section", "expert", None, "dp"),
        P("section", "expert", None, None, None),
        P("section", "expert", None, None, None),
    )
    return jax.shard_map(
        layer,
        mesh=mesh,
        in_specs=placed,
        out_specs=(P("section", "expert", "dp"), P("section", "expert", None)),
        check_vma=False,
    )
```

time: 59.2 us -> 51.9 us (0.88)
  the two profiles are of different devices: /device:TPU:1 before, /device:TPU:0 now
where the time goes in v2:
time: 51.9 us; the launch traced here: 51.7 us
  starting transfers between devices  21.7 us (42%)
  waiting for transfers between devices  18.7 us (36%)
  Pallas kernels  10.4 us (20%)
  between operations  0.83 us (2%)
    ppermute x15, starting transfers between devices, moved(): return lax.ppermute(value, AXES, device_pairs(route))  21.7 us
    ppermute x15, waiting for transfers between devices, moved(): return lax.ppermute(value, AXES, device_pairs(route))  18.7 us
    pallas_call x11, Pallas kernels, kernel_call(): pl.pallas_call(body, out_shape=outs, in_specs=[pl.BlockSpec(memory_space=...  10.4 us
  transfers between devices with their start and end apart: 15, of which 7 were waited for; matrix products, arithmetic and copies ran while one was open for 0% of the time, Pallas kernels for 15%

profile of v2, /device:TPU:0, one launch (start us, length us, event | category | flops | bytes accessed | tf_op | source)
XLA Modules:
  0.0 51.7 jit_solution(7077185397207582333)
XLA Ops:
  0.6 1.3 %shard_map.95 = (bf16[48,1024]{1,0:T(8,128)(2,1)S(1)}, bf16[48,1024]{1,0:T(8,128)(2,1)S(1)}, bf16[48,1024]{1,0:T(8,128)(2,1)S(1)}, bf16[48,1024]{1,0:T(8,128)(2,...) custom-call(s32[1]{0:T(128)} %bitcast.1.expert_ref, s32[2,64]{1,0:T(2,128)} %bitcast.25, ...), custom_call_target="tpu_custom_call" | custom-call | flops 25165824 | bytes 131844 | tf_op jit(solution)/shard_map/pallas_call | solution.py:49
  1.9 3.1 %collective-permute-start = (bf16[48,1024]{1,0:T(8,128)(2,1)S(1)}, bf16[48,1024]{1,0:T(8,128)(2,1)S(1)}, u32[]{:S(2)}, u32[]{:S(2)}) collective-permute-start(bf16[48,1024]{1,0:T(8,128)(2,1)S(1)} %get-tuple-element.22), channel_id=1, source_target_pairs={{0,1},{1,0},{2,3},{3,2},{4,5},{5,4},{6,7},{7,6},{8,9},{9,8},{10,11... | collective-permute-start | bytes 294920 | tf_op jit(solution)/shard_map/ppermute | solution.py:31
  5.0 2.5 %shard_map.96 = (bf16[768,1024]{1,0:T(8,128)(2,1)S(1)}, bf16[1024,768]{1,0:T(8,128)(2,1)S(1)}, bf16[1024,768]{1,0:T(8,128)(2,1)S(1)}, bf16[4,48,768]{2,1,0:T(8,128)(2,1)S(1)}, bf16[4,48,768]{2,1,0:T(8,128)(2,1)S(1)}) custom-call(bf16[768,1024]{1,0:T(8,128)(2,1)} %bitcast.19, bf16[1024,768]{1,0:T(8,128)(2,1)} %bitcast.20, bf16[1024,768]{1,0:T(8,128)(2,1)} %bitcast.21, ...), custom_call_target="tpu_custom_call" | custom-call | bytes 5308416 | tf_op jit(solution)/shard_map/pallas_call | solution.py:49
  7.5 0.3 collective-permute-done.refs_1_
  7.8 0.6 %shard_map.97 = bf16[96,768]{1,0:T(8,128)(2,1)S(1)} custom-call(bf16[48,1024]{1,0:T(8,128)(2,1)S(1)} %get-tuple-element.21.refs_0_, bf16[48,1024]{1,0:T(8,128)(2,1)S(1)} %collective-permute-done.refs_1_, bf16[768,1024]{1,0:T(8,128)(2,1)S(1)} %get-tuple-element.23.refs_2_.refs_1_), custom_call_target="tpu_custom_call" | custom-call | flops 150994944 | bytes 1769472 | tf_op jit(solution)/shard_map/pallas_call | solution.py:49
  8.5 2.9 %collective-permute-start.5 = (bf16[48,1024]{1,0:T(8,128)(2,1)S(1)}, bf16[48,1024]{1,0:T(8,128)(2,1)S(1)}, u32[]{:S(2)}, u32[]{:S(2)}) collective-permute-start(bf16[48,1024]{1,0:T(8,128)(2,1)S(1)} %get-tuple-element.30), channel_id=1, source_target_pairs={{0,2},{1,3},{2,0},{3,1},{4,6},{5,7},{6,4},{7,5},{8,10},{9,11},{10,... | collective-permute-start | bytes 294920 | tf_op jit(solution)/shard_map/ppermute | solution.py:31
  11.4 1.4 %collective-permute-start.9 = (bf16[48,1024]{1,0:T(8,128)(2,1)S(1)}, bf16[48,1024]{1,0:T(8,128)(2,1)S(1)}, u32[]{:S(2)}, u32[]{:S(2)}) collective-permute-start(bf16[48,1024]{1,0:T(8,128)(2,1)S(1)} %get-tuple-element.32), channel_id=1, source_target_pairs={{0,3},{1,2},{2,1},{3,0},{4,7},{5,6},{6,5},{7,4},{8,11},{9,10},{10,... | collective-permute-start | bytes 294920 | tf_op jit(solution)/shard_map/ppermute | solution.py:31
  12.7 6.6 %collective-permute-done.5.refs_0_ = bf16[48,1024]{1,0:T(8,128)(2,1)S(1)} collective-permute-done((bf16[48,1024]{1,0:T(8,128)(2,1)S(1)}, bf16[48,1024]{1,0:T(8,128)(2,1)S(1)}, u32[]{:S(2)}, u32[]{:S(2)}) %collective-permute-start.5) | collective-permute-done | bytes 98336 | tf_op jit(solution)/shard_map/ppermute | solution.py:31
  19.3 0.5 %shard_map.100 = bf16[48,768]{1,0:T(8,128)(2,1)S(1)} custom-call(bf16[48,1024]{1,0:T(8,128)(2,1)S(1)} %collective-permute-done.5.refs_0_, bf16[768,1024]{1,0:T(8,128)(2,1)S(1)} %get-tuple-element.23.refs_2_.refs_1_), custom_call_target="tpu_custom_call" | custom-call | flops 75497472 | bytes 1671168 | tf_op jit(solution)/shard_map/pallas_call | solution.py:49
  19.9 0.1 collective-permute-start.6
  20.0 0.5 %shard_map.102 = bf16[48,768]{1,0:T(8,128)(2,1)S(1)} custom-call(bf16[48,1024]{1,0:T(8,128)(2,1)S(1)} %collective-permute-done.9.refs_0_, bf16[768,1024]{1,0:T(8,128)(2,1)S(1)} %get-tuple-element.23.refs_2_.refs_1_), custom_call_target="tpu_custom_call" | custom-call | flops 75497472 | bytes 1671168 | tf_op jit(solution)/shard_map/pallas_call | solution.py:49
  20.6 0.6 %collective-permute-start.10 = (bf16[48,768]{1,0:T(8,128)(2,1)S(1)}, bf16[48,768]{1,0:T(8,128)(2,1)S(1)}, u32[]{:S(2)}, u32[]{:S(2)}) collective-permute-start(bf16[48,768]{1,0:T(8,128)(2,1)S(1)} %shard_map.102), channel_id=1, source_target_pairs={{0,4},{1,5},{2,6},{3,7},{4,0},{5,1},{6,2},{7,3},{8,12},{9,13},{10,... | collective-permute-start | bytes 221192 | tf_op jit(solution)/shard_map/ppermute | solution.py:31
  21.2 1.8 %collective-permute-start.2 = (bf16[96,768]{1,0:T(8,128)(2,1)S(1)}, bf16[96,768]{1,0:T(8,128)(2,1)S(1)}, u32[]{:S(2)}, u32[]{:S(2)}) collective-permute-start(bf16[96,768]{1,0:T(8,128)(2,1)S(1)} %add_convert_fusion.here_ref), channel_id=1, source_target_pairs={{0,8},{1,9},{2,10},{3,11},{4,12},{5,13},{6,14},{7,15},{8,0},{9,1},... | collective-permute-start | bytes 442376 | tf_op jit(solution)/shard_map/ppermute | solution.py:31
  23.0 0.9 %collective-permute-start.11 = (bf16[48,768]{1,0:T(8,128)(2,1)S(1)}, bf16[48,768]{1,0:T(8,128)(2,1)S(1)}, u32[]{:S(2)}, u32[]{:S(2)}) collective-permute-start(bf16[48,768]{1,0:T(8,128)(2,1)S(1)} %add_convert_fusion.1.here_ref), channel_id=1, source_target_pairs={{0,8},{1,9},{2,10},{3,11},{4,12},{5,13},{6,14},{7,15},{8,0},{9,1},... | collective-permute-start | bytes 221192 | tf_op jit(solution)/shard_map/ppermute | solution.py:31
  23.9 3.9 %collective-permute-done.2.other_ref = bf16[96,768]{1,0:T(8,128)(2,1)S(1)} collective-permute-done((bf16[96,768]{1,0:T(8,128)(2,1)S(1)}, bf16[96,768]{1,0:T(8,128)(2,1)S(1)}, u32[]{:S(2)}, u32[]{:S(2)}) %collective-permute-start.2) | collective-permute-done | bytes 147488 | tf_op jit(solution)/shard_map/ppermute | solution.py:31
  27.8 1.1 %shard_map.98 = (bf16[48,1024]{1,0:T(8,128)(2,1)S(1)}, bf16[48,128]{1,0:T(8,128)(2,1)S(1)}, bf16[48,1152]{1,0:T(8,128)(2,1)S(1)}) custom-call(s32[1]{0:T(128)} %bitcast.1.expert_ref, bf16[96,768]{1,0:T(8,128)(2,1)S(1)} %add_convert_fusion.here_ref, bf16[96,768]{1,0:T(8,128)(2,1)S(1)} %collective-permute-done.2.other_ref, ...), custom_call_target="tpu_custom_call" | custom-call | flops 301989888 | bytes 4030468 | tf_op jit(solution)/shard_map/pallas_call | solution.py:49
  28.9 1.6 %collective-permute-start.3 = (bf16[48,1152]{1,0:T(8,128)(2,1)S(1)}, bf16[48,1152]{1,0:T(8,128)(2,1)S(1)}, u32[]{:S(2)}, u32[]{:S(2)}) collective-permute-start(bf16[48,1152]{1,0:T(8,128)(2,1)S(1)} %get-tuple-element.29), channel_id=1, source_target_pairs={{0,1},{1,0},{2,3},{3,2},{4,5},{5,4},{6,7},{7,6},{8,9},{9,8},{10,11... | collective-permute-start | bytes 331784 | tf_op jit(solution)/shard_map/ppermute | solution.py:31
  30.6 1.6 %collective-permute-start.7 = (bf16[48,768]{1,0:T(8,128)(2,1)S(1)}, bf16[48,768]{1,0:T(8,128)(2,1)S(1)}, u32[]{:S(2)}, u32[]{:S(2)}) collective-permute-start(bf16[48,768]{1,0:T(8,128)(2,1)S(1)} %add_convert_fusion.2.here_ref), channel_id=1, source_target_pairs={{0,8},{1,9},{2,10},{3,11},{4,12},{5,13},{6,14},{7,15},{8,0},{9,1},... | collective-permute-start | bytes 221192 | tf_op jit(solution)/shard_map/ppermute | solution.py:31
  32.1 1.6 %collective-permute-done.3.refs_0_.refs_1_ = bf16[48,1152]{1,0:T(8,128)(2,1)S(1)} collective-permute-done((bf16[48,1152]{1,0:T(8,128)(2,1)S(1)}, bf16[48,1152]{1,0:T(8,128)(2,1)S(1)}, u32[]{:S(2)}, u32[]{:S(2)}) %collective-permute-start.3) | collective-permute-done | bytes 110624 | tf_op jit(solution)/shard_map/ppermute | solution.py:31
  33.7 0.2 shard_map.99
  34.0 1.3 %collective-permute-start.4 = (bf16[64,1120]{1,0:T(8,128)(2,1)S(1)}, bf16[64,1120]{1,0:T(8,128)(2,1)S(1)}, u32[]{:S(2)}, u32[]{:S(2)}) collective-permute-start(bf16[64,1120]{1,0:T(8,128)(2,1)S(1)} %shard_map.99), channel_id=1, source_target_pairs={{16,0},{17,1},{18,2},{19,3},{20,4},{21,5},{22,6},{23,7},{24,8},{25... | collective-permute-start | bytes 430088 | tf_op jit(solution)/shard_map/ppermute | solution.py:31
  35.3 1.0 %shard_map.103 = (bf16[48,1024]{1,0:T(8,128)(2,1)S(1)}, bf16[48,128]{1,0:T(8,128)(2,1)S(1)}) custom-call(s32[1]{0:T(128)} %bitcast.1.expert_ref, bf16[48,768]{1,0:T(8,128)(2,1)S(1)} %add_convert_fusion.1.here_ref, bf16[48,768]{1,0:T(8,128)(2,1)S(1)} %collective-permute-done.11.other_ref, bf16[4,48,768]{2,1,0:T(8,128)(2,1)S(1)} %get-tuple-element.24.saved_gate_ref, ...), custom_call_target="tpu_custom_call" | custom-call | flops 150994944 | bytes 3883012 | tf_op jit(solution)/shard_map/pallas_call | solution.py:49
  36.3 1.3 %collective-permute-start.12 = (bf16[48,1024]{1,0:T(8,128)(2,1)S(1)}, bf16[48,1024]{1,0:T(8,128)(2,1)S(1)}, u32[]{:S(2)}, u32[]{:S(2)}) collective-permute-start(bf16[48,1024]{1,0:T(8,128)(2,1)S(1)} %get-tuple-element.33), channel_id=1, source_target_pairs={{16,3},{17,2},{18,1},{19,0},{20,7},{21,6},{22,5},{23,4},{24,11},{2... | collective-permute-start | bytes 294920 | tf_op jit(solution)/shard_map/ppermute | solution.py:31
  37.6 1.0 %shard_map.101 = (bf16[48,1024]{1,0:T(8,128)(2,1)S(1)}, bf16[48,128]{1,0:T(8,128)(2,1)S(1)}) custom-call(s32[1]{0:T(128)} %bitcast.1.expert_ref, bf16[48,768]{1,0:T(8,128)(2,1)S(1)} %add_convert_fusion.2.here_ref, bf16[48,768]{1,0:T(8,128)(2,1)S(1)} %collective-permute-done.7.other_ref, bf16[4,48,768]{2,1,0:T(8,128)(2,1)S(1)} %get-tuple-element.24.saved_gate_ref, ...), custom_call_target="tpu_custom_call" | custom-call | flops 150994944 | bytes 3883012 | tf_op jit(solution)/shard_map/pallas_call | solution.py:49
  38.7 1.3 %collective-permute-start.8 = (bf16[48,1024]{1,0:T(8,128)(2,1)S(1)}, bf16[48,1024]{1,0:T(8,128)(2,1)S(1)}, u32[]{:S(2)}, u32[]{:S(2)}) collective-permute-start(bf16[48,1024]{1,0:T(8,128)(2,1)S(1)} %get-tuple-element.31), channel_id=1, source_target_pairs={{16,2},{17,3},{18,0},{19,1},{20,6},{21,7},{22,4},{23,5},{24,10},{2... | collective-permute-start | bytes 294920 | tf_op jit(solution)/shard_map/ppermute | solution.py:31
  40.0 3.5 %collective-permute-start.13 = (bf16[48,128]{1,0:T(8,128)(2,1)S(1)}, bf16[48,128]{1,0:T(8,128)(2,1)S(1)}, u32[]{:S(2)}, u32[]{:S(2)}) collective-permute-start(bf16[48,128]{1,0:T(8,128)(2,1)S(1)} %get-tuple-element.36), channel_id=1, source_target_pairs={{0,2},{1,3},{2,0},{3,1},{4,6},{5,7},{6,4},{7,5},{8,10},{9,11},{10,... | collective-permute-start | bytes 36872 | tf_op jit(solution)/shard_map/ppermute | solution.py:31
  43.5 0.4 collective-permute-start.14
  44.0 1.2 %collective-permute-done.13.refs_2_ = bf16[48,128]{1,0:T(8,128)(2,1)S(1)} collective-permute-done((bf16[48,128]{1,0:T(8,128)(2,1)S(1)}, bf16[48,128]{1,0:T(8,128)(2,1)S(1)}, u32[]{:S(2)}, u32[]{:S(2)}) %collective-permute-start.13) | collective-permute-done | bytes 12320 | tf_op jit(solution)/shard_map/ppermute | solution.py:31
  45.2 3.8 %collective-permute-done.14.refs_3_ = bf16[48,128]{1,0:T(8,128)(2,1)S(1)} collective-permute-done((bf16[48,128]{1,0:T(8,128)(2,1)S(1)}, bf16[48,128]{1,0:T(8,128)(2,1)S(1)}, u32[]{:S(2)}, u32[]{:S(2)}) %collective-permute-start.14) | collective-permute-done | bytes 12320 | tf_op jit(solution)/shard_map/ppermute | solution.py:31
  49.0 0.7 %shard_map.105 = bf16[2,64]{1,0:T(2,128)(2,1)} custom-call(bf16[2,192,64]{2,1,0:T(8,128)(2,1)S(1)} %get-tuple-element.34.hold_ref, bf16[48,128]{1,0:T(8,128)(2,1)S(1)} %get-tuple-element.35.refs_0_, bf16[48,1152]{1,0:T(8,128)(2,1)S(1)} %collective-permute-done.3.refs_0_.refs_1_, bf16[48,128]{1,0:T(8,128)(2,1)S(1)} %collective-permute-done.13.refs_2_, ...), custom_call_target="tpu_custom_call" | custom-call | bytes 196608 | tf_op jit(solution)/shard_map/pallas_call | solution.py:49
  49.7 1.2 %collective-permute-done.8.refs_0_ = bf16[48,1024]{1,0:T(8,128)(2,1)S(1)} collective-permute-done((bf16[48,1024]{1,0:T(8,128)(2,1)S(1)}, bf16[48,1024]{1,0:T(8,128)(2,1)S(1)}, u32[]{:S(2)}, u32[]{:S(2)}) %collective-permute-start.8) | collective-permute-done | bytes 98336 | tf_op jit(solution)/shard_map/ppermute | solution.py:31
  50.9 0.8 %shard_map.104 = bf16[64,1024]{1,0:T(8,128)(2,1)} custom-call(bf16[64,1120]{1,0:T(8,128)(2,1)S(1)} %collective-permute-done.4.message_ref, bf16[48,1024]{1,0:T(8,128)(2,1)S(1)} %collective-permute-done.8.refs_0_, bf16[48,1024]{1,0:T(8,128)(2,1)S(1)} %collective-permute-done.12.refs_1_), custom_call_target="tpu_custom_call" | custom-call | flops 12582912 | bytes 339968 | tf_op jit(solution)/shard_map/pallas_call | solution.py:49
  (14 shorter events, 0.2 us)
Async XLA Ops:
  1.9 5.9 %collective-permute-start = (bf16[48,1024]{1,0:T(8,128)(2,1)S(1)}, bf16[48,1024]{1,0:T(8,128)(2,1)S(1)}, u32[]{:S(2)}, u32[]{:S(2)}) collective-permute-start(bf16[48,1024]{1,0:T(8,128)(2,1)S(1)} %get-tuple-element.22), channel_id=1, source_target_pairs={{0,1},{1,0},{2,3},{3,2},{4,5},{5,4},{6,7},{7,6},{8,9},{9,8},{10,11... | collective-permute-start | bytes 294920 | tf_op jit(solution)/shard_map/ppermute | solution.py:31
  8.4 12.7 %collective-permute-start.1 = (bf16[96,768]{1,0:T(8,128)(2,1)S(1)}, bf16[96,768]{1,0:T(8,128)(2,1)S(1)}, u32[]{:S(2)}, u32[]{:S(2)}) collective-permute-start(bf16[96,768]{1,0:T(8,128)(2,1)S(1)} %shard_map.97), channel_id=1, source_target_pairs={{0,4},{1,5},{2,6},{3,7},{4,0},{5,1},{6,2},{7,3},{8,12},{9,13},{10,... | collective-permute-start | bytes 442376 | tf_op jit(solution)/shard_map/ppermute | solution.py:31
  8.5 10.8 %collective-permute-start.5 = (bf16[48,1024]{1,0:T(8,128)(2,1)S(1)}, bf16[48,1024]{1,0:T(8,128)(2,1)S(1)}, u32[]{:S(2)}, u32[]{:S(2)}) collective-permute-start(bf16[48,1024]{1,0:T(8,128)(2,1)S(1)} %get-tuple-element.30), channel_id=1, source_target_pairs={{0,2},{1,3},{2,0},{3,1},{4,6},{5,7},{6,4},{7,5},{8,10},{9,11},{10,... | collective-permute-start | bytes 294920 | tf_op jit(solution)/shard_map/ppermute | solution.py:31
  11.4 8.6 %collective-permute-start.9 = (bf16[48,1024]{1,0:T(8,128)(2,1)S(1)}, bf16[48,1024]{1,0:T(8,128)(2,1)S(1)}, u32[]{:S(2)}, u32[]{:S(2)}) collective-permute-start(bf16[48,1024]{1,0:T(8,128)(2,1)S(1)} %get-tuple-element.32), channel_id=1, source_target_pairs={{0,3},{1,2},{2,1},{3,0},{4,7},{5,6},{6,5},{7,4},{8,11},{9,10},{10,... | collective-permute-start | bytes 294920 | tf_op jit(solution)/shard_map/ppermute | solution.py:31
  19.9 10.6 %collective-permute-start.6 = (bf16[48,768]{1,0:T(8,128)(2,1)S(1)}, bf16[48,768]{1,0:T(8,128)(2,1)S(1)}, u32[]{:S(2)}, u32[]{:S(2)}) collective-permute-start(bf16[48,768]{1,0:T(8,128)(2,1)S(1)} %shard_map.100), channel_id=1, source_target_pairs={{0,4},{1,5},{2,6},{3,7},{4,0},{5,1},{6,2},{7,3},{8,12},{9,13},{10,... | collective-permute-start | bytes 221192 | tf_op jit(solution)/shard_map/ppermute | solution.py:31
  20.6 2.4 %collective-permute-start.10 = (bf16[48,768]{1,0:T(8,128)(2,1)S(1)}, bf16[48,768]{1,0:T(8,128)(2,1)S(1)}, u32[]{:S(2)}, u32[]{:S(2)}) collective-permute-start(bf16[48,768]{1,0:T(8,128)(2,1)S(1)} %shard_map.102), channel_id=1, source_target_pairs={{0,4},{1,5},{2,6},{3,7},{4,0},{5,1},{6,2},{7,3},{8,12},{9,13},{10,... | collective-permute-start | bytes 221192 | tf_op jit(solution)/shard_map/ppermute | solution.py:31
  21.2 6.6 %collective-permute-start.2 = (bf16[96,768]{1,0:T(8,128)(2,1)S(1)}, bf16[96,768]{1,0:T(8,128)(2,1)S(1)}, u32[]{:S(2)}, u32[]{:S(2)}) collective-permute-start(bf16[96,768]{1,0:T(8,128)(2,1)S(1)} %add_convert_fusion.here_ref), channel_id=1, source_target_pairs={{0,8},{1,9},{2,10},{3,11},{4,12},{5,13},{6,14},{7,15},{8,0},{9,1},... | collective-permute-start | bytes 442376 | tf_op jit(solution)/shard_map/ppermute | solution.py:31
  23.0 12.3 %collective-permute-start.11 = (bf16[48,768]{1,0:T(8,128)(2,1)S(1)}, bf16[48,768]{1,0:T(8,128)(2,1)S(1)}, u32[]{:S(2)}, u32[]{:S(2)}) collective-permute-start(bf16[48,768]{1,0:T(8,128)(2,1)S(1)} %add_convert_fusion.1.here_ref), channel_id=1, source_target_pairs={{0,8},{1,9},{2,10},{3,11},{4,12},{5,13},{6,14},{7,15},{8,0},{9,1},... | collective-permute-start | bytes 221192 | tf_op jit(solution)/shard_map/ppermute | solution.py:31
  27.8 5.9 %copy-start = (bf16[1,64,1024]{2,1,0:T(8,128)(2,1)S(1)}, bf16[1,64,1024]{2,1,0:T(8,128)(2,1)}, u32[]{:S(2)}) copy-start(bf16[1,64,1024]{2,1,0:T(8,128)(2,1)} %param.8) | copy-start | bytes 393220
  28.9 4.8 %collective-permute-start.3 = (bf16[48,1152]{1,0:T(8,128)(2,1)S(1)}, bf16[48,1152]{1,0:T(8,128)(2,1)S(1)}, u32[]{:S(2)}, u32[]{:S(2)}) collective-permute-start(bf16[48,1152]{1,0:T(8,128)(2,1)S(1)} %get-tuple-element.29), channel_id=1, source_target_pairs={{0,1},{1,0},{2,3},{3,2},{4,5},{5,4},{6,7},{7,6},{8,9},{9,8},{10,11... | collective-permute-start | bytes 331784 | tf_op jit(solution)/shard_map/ppermute | solution.py:31
  30.6 7.1 %collective-permute-start.7 = (bf16[48,768]{1,0:T(8,128)(2,1)S(1)}, bf16[48,768]{1,0:T(8,128)(2,1)S(1)}, u32[]{:S(2)}, u32[]{:S(2)}) collective-permute-start(bf16[48,768]{1,0:T(8,128)(2,1)S(1)} %add_convert_fusion.2.here_ref), channel_id=1, source_target_pairs={{0,8},{1,9},{2,10},{3,11},{4,12},{5,13},{6,14},{7,15},{8,0},{9,1},... | collective-permute-start | bytes 221192 | tf_op jit(solution)/shard_map/ppermute | solution.py:31
  34.0 16.9 %collective-permute-start.4 = (bf16[64,1120]{1,0:T(8,128)(2,1)S(1)}, bf16[64,1120]{1,0:T(8,128)(2,1)S(1)}, u32[]{:S(2)}, u32[]{:S(2)}) collective-permute-start(bf16[64,1120]{1,0:T(8,128)(2,1)S(1)} %shard_map.99), channel_id=1, source_target_pairs={{16,0},{17,1},{18,2},{19,3},{20,4},{21,5},{22,6},{23,7},{24,8},{25... | collective-permute-start | bytes 430088 | tf_op jit(solution)/shard_map/ppermute | solution.py:31
  36.3 13.4 %collective-permute-start.12 = (bf16[48,1024]{1,0:T(8,128)(2,1)S(1)}, bf16[48,1024]{1,0:T(8,128)(2,1)S(1)}, u32[]{:S(2)}, u32[]{:S(2)}) collective-permute-start(bf16[48,1024]{1,0:T(8,128)(2,1)S(1)} %get-tuple-element.33), channel_id=1, source_target_pairs={{16,3},{17,2},{18,1},{19,0},{20,7},{21,6},{22,5},{23,4},{24,11},{2... | collective-permute-start | bytes 294920 | tf_op jit(solution)/shard_map/ppermute | solution.py:31
  38.7 12.2 %collective-permute-start.8 = (bf16[48,1024]{1,0:T(8,128)(2,1)S(1)}, bf16[48,1024]{1,0:T(8,128)(2,1)S(1)}, u32[]{:S(2)}, u32[]{:S(2)}) collective-permute-start(bf16[48,1024]{1,0:T(8,128)(2,1)S(1)} %get-tuple-element.31), channel_id=1, source_target_pairs={{16,2},{17,3},{18,0},{19,1},{20,6},{21,7},{22,4},{23,5},{24,10},{2... | collective-permute-start | bytes 294920 | tf_op jit(solution)/shard_map/ppermute | solution.py:31
  40.0 5.2 %collective-permute-start.13 = (bf16[48,128]{1,0:T(8,128)(2,1)S(1)}, bf16[48,128]{1,0:T(8,128)(2,1)S(1)}, u32[]{:S(2)}, u32[]{:S(2)}) collective-permute-start(bf16[48,128]{1,0:T(8,128)(2,1)S(1)} %get-tuple-element.36), channel_id=1, source_target_pairs={{0,2},{1,3},{2,0},{3,1},{4,6},{5,7},{6,4},{7,5},{8,10},{9,11},{10,... | collective-permute-start | bytes 36872 | tf_op jit(solution)/shard_map/ppermute | solution.py:31
  43.5 5.5 %collective-permute-start.14 = (bf16[48,128]{1,0:T(8,128)(2,1)S(1)}, bf16[48,128]{1,0:T(8,128)(2,1)S(1)}, u32[]{:S(2)}, u32[]{:S(2)}) collective-permute-start(bf16[48,128]{1,0:T(8,128)(2,1)S(1)} %get-tuple-element.37), channel_id=1, source_target_pairs={{0,3},{1,2},{2,1},{3,0},{4,7},{5,6},{6,5},{7,4},{8,11},{9,10},{10,... | collective-permute-start | bytes 36872 | tf_op jit(solution)/shard_map/ppermute | solution.py:31

commit v3 on v2

--- a/solution.py
+++ b/solution.py
@@ -57,7 +57,7 @@
     )(*ins)
 
 
-def table_kernel(capacity, experts, expert_ref, route_hbm, gate_hbm, grads_hbm, *refs):
+def table_kernel(capacity, experts, route_hbm, gate_hbm, grads_hbm, *refs):
     row_refs, (gated_ref, hold_ref) = (refs[:experts], refs[experts : experts + 2])
     route_ref, gate_ref, grads_ref, semaphores = refs[experts + 2 :]
     copies = [
@@ -73,7 +73,7 @@
     place = lax.broadcasted_iota(jnp.int32, (slots, 1), 0)
     block = lax.div(place, capacity)
     inside = (place - block * capacity).astype(jnp.float32)
-    label = expert_ref[0] ^ block
+    label = lax.axis_index("expert") ^ block
     row = lax.broadcasted_iota(jnp.int32, (tokens, tokens), 0)
     column = lax.broadcasted_iota(jnp.int32, (tokens, tokens), 1)
     before = jnp.where(row < column, 1.0, 0.0).astype(jnp.bfloat16)
@@ -97,16 +97,10 @@
     gated_ref[...] = gated.astype(jnp.bfloat16)
 
 
-def fetch_kernel(*refs):
-    count = len(refs) // 2
-    copies = [
-        pltpu.make_async_copy(refs[index], refs[count + index], refs[-1].at[index])
-        for index in range(count)
-    ]
-    for copy in copies:
-        copy.start()
-    for copy in copies:
-        copy.wait()
+def fetch_kernel(source_ref, target_ref, semaphore):
+    copy = pltpu.make_async_copy(source_ref, target_ref, semaphore)
+    copy.start()
+    copy.wait()
 
 
 def raw_kernel(*refs):
@@ -115,11 +109,11 @@
     out_ref[...] = matmul_t(rows, down_ref[...]).astype(jnp.bfloat16)
 
 
-def back_kernel(offsets, capacity, near, expert_ref, here_ref, other_ref, saved_gate_ref, saved_up_ref, gate_ref, up_ref, *refs):
+def back_kernel(offsets, capacity, name, here_ref, other_ref, saved_gate_ref, saved_up_ref, gate_ref, up_ref, *refs):
     total = here_ref[...].astype(jnp.float32) + other_ref[...].astype(jnp.float32)
 
     def picked(ref):
-        return jnp.concatenate([ref[expert_ref[0] ^ k] for k in offsets]).astype(jnp.float32)
+        return jnp.concatenate([ref[lax.axis_index("expert") ^ k] for k in offsets]).astype(jnp.float32)
 
     gate_val, up_val = (picked(saved_gate_ref), picked(saved_up_ref))
     sigmoid_val = jax.nn.sigmoid(gate_val)
@@ -134,16 +128,22 @@
         jnp.bfloat16
     )
     inner = jnp.broadcast_to(inner, (inner.shape[0], 128)).astype(jnp.bfloat16)
+    count = len(offsets)
+    if name == "b":
+        earlier, refs = (refs[:count], refs[count:])
+        first = (lax.axis_index("dp") & 1) == 0
     outs = iter(refs)
     for index, k in enumerate(offsets):
         own = slice(index * capacity, (index + 1) * capacity)
-        if near and k:
+        if name == "c" and k:
             joined = next(outs)
             joined[:, : back.shape[1]] = back[own]
             joined[:, back.shape[1] :] = inner[own]
         else:
             next(outs)[...] = back[own]
-            next(outs)[...] = inner[own]
+            next(outs)[...] = (
+                jnp.where(first, earlier[index][...], inner[own]) if name == "b" else inner[own]
+            )
 
 
 def partial_kernel(grads_ref, gated_ref, first_ref, *refs):
@@ -161,24 +161,33 @@
     message_ref[:, width:] = matmul_t(same, gated_ref[near:]).astype(jnp.bfloat16)
 
 
-def combine_kernel(message_ref, *refs):
-    row_refs, out_ref = (refs[:-1], refs[-1])
-    width = out_ref.shape[1]
-    rows = jnp.concatenate([ref[...] for ref in row_refs])
-    gated = message_ref[:, width:]
-    out_ref[...] = (
-        message_ref[:, :width].astype(jnp.float32) + matmul(gated, rows)
-    ).astype(jnp.bfloat16)
-
-
-def gates_kernel(hold_ref, *refs):
-    slot_refs, out_ref = (refs[:-1], refs[-1])
-    slots = jnp.concatenate([ref[:, ref.shape[1] - 128 :] for ref in slot_refs])
+def finish_kernel(far, message_ref, hold_ref, *refs):
+    count = len(far)
+    row_refs, slot_refs, (handed_ref, gates_ref) = (refs[:count], refs[count:-2], refs[-2:])
+    near_refs, near_slots, other_slots = (
+        slot_refs[:-count],
+        slot_refs[-count : -(count // 2)],
+        slot_refs[-(count // 2) :],
+    )
+    first = (lax.axis_index("dp") & 1) == 0
+    found = {}
+    for index, (same, other) in enumerate(zip(near_slots, other_slots)):
+        found[far[index]] = jnp.where(first, same[...], other[...])
+        found[far[index + count // 2]] = jnp.where(first, other[...], same[...])
+    slots = jnp.concatenate(
+        [ref[:, ref.shape[1] - 128 :] for ref in near_refs] + [found[k] for k in sorted(far)]
+    )
     for pick in range(hold_ref.shape[0]):
         found = lax.dot_general(
             slots, hold_ref[pick], LEADING, preferred_element_type=jnp.float32
         )
-        out_ref[pick : pick + 1, :] = found[:1].astype(jnp.bfloat16)
+        gates_ref[pick : pick + 1, :] = found[:1].astype(jnp.bfloat16)
+    width = handed_ref.shape[1]
+    rows = jnp.concatenate([ref[...] for ref in row_refs])
+    gated = message_ref[:, width:]
+    handed = message_ref[:, :width].astype(jnp.float32) + matmul(gated, rows)
+    later = lax.axis_index("section") < lax.axis_size("section") - 1
+    handed_ref[...] = jnp.where(later, handed, 0.0).astype(jnp.bfloat16)
 
 
 def layer(upstream, routes, gate_weights, w_gate, w_up, w_down, saved_gate, saved_up):
@@ -190,7 +199,6 @@
     tokens, picks = route_block.shape
     width = grads_here.shape[1]
     units = w_down.shape[2]
-    expert_id = lax.axis_index("expert").astype(jnp.int32)[None]
     bf16 = lambda *shape: jax.ShapeDtypeStruct(shape, jnp.bfloat16)
 
     *rows, gated, holds = kernel_call(
@@ -200,9 +208,9 @@
             bf16(experts * capacity, tokens),
             bf16(picks, experts * capacity, tokens),
         ),
-        (expert_id, route_block.T, gate_weights[0].T, grads_here),
+        (route_block.T, gate_weights[0].T, grads_here),
         2 * experts * capacity * tokens * width,
-        [pltpu.SMEM] + [pltpu.HBM] * 3,
+        [pltpu.HBM] * 3,
         (
             pltpu.VMEM((picks, tokens), jnp.int32),
             pltpu.VMEM((picks, tokens), jnp.bfloat16),
@@ -211,11 +219,13 @@
         ),
     )
 
+    sections = lax.axis_size("section")
+
     def across(k, shift=0):
-        return lambda s, d, e: (s - shift, d, e ^ k) if s >= shift else None
+        return lambda s, d, e: ((s - shift) % sections, d, e ^ k)
 
     half = experts // 2
-    far = [k for k in range(half, experts)]
+    far = list(range(experts - 1, half - 1, -1))
     cut = (len(far) + 1) // 2
     chunks = {"a": far[:cut], "b": far[cut:], "c": list(range(half))}
     arrived = {0: rows[0]}
@@ -224,17 +234,17 @@
             if k:
                 arrived[k] = moved(rows[k], across(k))
 
-    held = (w_down[0, 0], w_gate[0, 0], w_up[0, 0], saved_gate[0, 0], saved_up[0, 0])
-    down, gate, up, gate_pre, up_pre = kernel_call(
+    gate, up, gate_pre, up_pre = (w_gate[0, 0], w_up[0, 0], saved_gate[0, 0], saved_up[0, 0])
+    down = kernel_call(
         fetch_kernel,
-        tuple(bf16(*value.shape) for value in held),
-        held,
+        bf16(units, width),
+        (w_down[0, 0],),
         0,
-        [pltpu.HBM] * len(held),
-        (pltpu.SemaphoreType.DMA((len(held),)),),
+        [pltpu.HBM],
+        (pltpu.SemaphoreType.DMA,),
     )
     row_grad, slot_grad = ({}, {})
-    for name in ("a", "b", "c"):
+    for name in ("c", "a", "b"):
         chosen = chunks[name]
         count = len(chosen) * capacity
         total = kernel_call(
@@ -249,25 +259,24 @@
             distance *= 2
             if distance < parts:
                 total = (total.astype(jnp.float32) + other.astype(jnp.float32)).astype(jnp.bfloat16)
-        near = name == "c"
         outs = []
         for k in chosen:
-            if near and k:
+            if name == "c" and k:
                 outs.append(bf16(capacity, width + 128))
             else:
                 outs.extend([bf16(capacity, width), bf16(capacity, 128)])
         results = list(
             kernel_call(
-                functools.partial(back_kernel, tuple(chosen), capacity, near),
+                functools.partial(back_kernel, tuple(chosen), capacity, name),
                 tuple(outs),
-                (expert_id, total, other, gate_pre, up_pre, gate, up),
+                (total, other, gate_pre, up_pre, gate, up)
+                + (tuple(slot_grad[k] for k in chunks["a"]) if name == "b" else ()),
                 4 * count * width * units,
-                [pltpu.SMEM] + [pltpu.VMEM] * 6,
             )
         )
         for k in chosen:
             row_grad[k] = results.pop(0)
-            if not (near and k):
+            if not (name == "c" and k):
                 slot_grad[k] = results.pop(0)
 
     returned = {}
@@ -281,17 +290,23 @@
         (grads_here, gated, row_grad[0], *[returned[k] for k in range(1, half)]),
         2 * tokens * width * half * capacity,
     )
-    message = moved(message, lambda s, d, e: (s - 1, d, e) if s >= 1 else None)
-    handed = kernel_call(
-        combine_kernel,
-        bf16(tokens, width),
-        (message, *[returned[k] for k in far]),
+    message = moved(message, across(0, 1))
+    slot_back = [slot_grad[0], *[returned[k] for k in range(1, half)]]
+    mine = []
+    for first, second in zip(chunks["a"], chunks["b"]):
+        mine.append(
+            moved(
+                slot_grad[second],
+                lambda s, d, e, k=(first, second): (s, d, e ^ k[d & 1]),
+            )
+        )
+    slot_back += mine + [moved(value, lambda s, d, e: (s, d ^ 1, e)) for value in mine]
+    handed, gate_grads = kernel_call(
+        functools.partial(finish_kernel, tuple(far)),
+        (bf16(tokens, width), bf16(picks, tokens)),
+        (message, holds, *[returned[k] for k in sorted(far)], *slot_back),
         2 * tokens * width * half * capacity,
     )
-    slot_back = [slot_grad[0], *[returned[k] for k in range(1, half)]]
-    for k in far:
-        slot_back.append(moved(slot_grad[k], across(k)))
-    gate_grads = kernel_call(gates_kernel, bf16(picks, tokens), (holds, *slot_back))
     return (handed[None], gate_grads.T[None])
 
 

time: 51.9 us -> 51 us (0.983)
  starting transfers between devices: 21.7 us -> 23.7 us
  Pallas kernels: 10.4 us -> 8.78 us
  waiting for transfers between devices: 18.7 us -> 17.5 us
    ppermute x15, starting transfers between devices: 21.7 us -> 23.7 us  [moved(): return lax.ppermute(value, AXES, device_pairs(route))]
    pallas_call x11 -> x10, Pallas kernels: 10.4 us -> 8.78 us  [kernel_call(): pl.pallas_call(body, out_shape=outs, in_specs=[pl.BlockSpec(memory_space=...]
    ppermute x15, waiting for transfers between devices: 18.7 us -> 17.5 us  [moved(): return lax.ppermute(value, AXES, device_pairs(route))]
  transfers between devices with their start and end apart: 15 -> 15, of which waited for: 7 -> 6; matrix products, arithmetic and copies ran while one was open for 0% -> 0% of each run, Pallas kernels for 15% -> 12%
where the time goes in v3:
time: 51 us; the launch traced here: 50.9 us
  starting transfers between devices  23.7 us (46%)
  waiting for transfers between devices  17.5 us (34%)
  Pallas kernels  8.78 us (17%)
  between operations  0.85 us (2%)
    ppermute x15, starting transfers between devices, moved(): return lax.ppermute(value, AXES, device_pairs(route))  23.7 us
    ppermute x15, waiting for transfers between devices, moved(): return lax.ppermute(value, AXES, device_pairs(route))  17.5 us
    pallas_call x10, Pallas kernels, kernel_call(): pl.pallas_call(body, out_shape=outs, in_specs=[pl.BlockSpec(memory_space=...  8.78 us
  transfers between devices with their start and end apart: 15, of which 6 were waited for; matrix products, arithmetic and copies ran while one was open for 0% of the time, Pallas kernels for 12%

profile of v3, /device:TPU:0, one launch (start us, length us, event | category | flops | bytes accessed | tf_op | source)
XLA Modules:
  0.0 50.9 jit_solution(10145677101920051584)
XLA Ops:
  0.6 1.3 %shard_map.95 = (bf16[48,1024]{1,0:T(8,128)(2,1)S(1)}, bf16[48,1024]{1,0:T(8,128)(2,1)S(1)}, bf16[48,1024]{1,0:T(8,128)(2,1)S(1)}, bf16[48,1024]{1,0:T(8,128)(2,...) custom-call(s32[2,64]{1,0:T(2,128)} %bitcast.31, bf16[2,64]{1,0:T(2,128)(2,1)} %bitcast.32, ...), custom_call_target="tpu_custom_call" | custom-call | flops 25165824 | bytes 131840 | tf_op jit(solution)/shard_map/pallas_call | solution.py:49
  1.9 3.1 %collective-permute-start = (bf16[48,1024]{1,0:T(8,128)(2,1)S(1)}, bf16[48,1024]{1,0:T(8,128)(2,1)S(1)}, u32[]{:S(2)}, u32[]{:S(2)}) collective-permute-start(bf16[48,1024]{1,0:T(8,128)(2,1)S(1)} %get-tuple-element.19), channel_id=1, source_target_pairs={{0,1},{1,0},{2,3},{3,2},{4,5},{5,4},{6,7},{7,6},{8,9},{9,8},{10,11... | collective-permute-start | bytes 294920 | tf_op jit(solution)/shard_map/ppermute | solution.py:31
  5.0 1.4 %shard_map.96.refs_2_.refs_1_ = bf16[768,1024]{1,0:T(8,128)(2,1)S(1)} custom-call(bf16[768,1024]{1,0:T(8,128)(2,1)} %bitcast.30), custom_call_target="tpu_custom_call" | custom-call | bytes 1572864 | tf_op jit(solution)/shard_map/pallas_call | solution.py:49
  6.4 1.4 %collective-permute-done.refs_1_ = bf16[48,1024]{1,0:T(8,128)(2,1)S(1)} collective-permute-done((bf16[48,1024]{1,0:T(8,128)(2,1)S(1)}, bf16[48,1024]{1,0:T(8,128)(2,1)S(1)}, u32[]{:S(2)}, u32[]{:S(2)}) %collective-permute-start) | collective-permute-done | bytes 98336 | tf_op jit(solution)/shard_map/ppermute | solution.py:31
  7.8 0.6 %shard_map.97 = bf16[96,768]{1,0:T(8,128)(2,1)S(1)} custom-call(bf16[48,1024]{1,0:T(8,128)(2,1)S(1)} %get-tuple-element.18.refs_0_, bf16[48,1024]{1,0:T(8,128)(2,1)S(1)} %collective-permute-done.refs_1_, bf16[768,1024]{1,0:T(8,128)(2,1)S(1)} %shard_map.96.refs_2_.refs_1_), custom_call_target="tpu_custom_call" | custom-call | flops 150994944 | bytes 1769472 | tf_op jit(solution)/shard_map/pallas_call | solution.py:49
  8.4 0.1 collective-permute-start.1
  8.5 2.9 %collective-permute-start.5 = (bf16[48,1024]{1,0:T(8,128)(2,1)S(1)}, bf16[48,1024]{1,0:T(8,128)(2,1)S(1)}, u32[]{:S(2)}, u32[]{:S(2)}) collective-permute-start(bf16[48,1024]{1,0:T(8,128)(2,1)S(1)} %get-tuple-element.23), channel_id=1, source_target_pairs={{0,2},{1,3},{2,0},{3,1},{4,6},{5,7},{6,4},{7,5},{8,10},{9,11},{10,... | collective-permute-start | bytes 294920 | tf_op jit(solution)/shard_map/ppermute | solution.py:31
  11.4 1.3 %collective-permute-start.8 = (bf16[48,1024]{1,0:T(8,128)(2,1)S(1)}, bf16[48,1024]{1,0:T(8,128)(2,1)S(1)}, u32[]{:S(2)}, u32[]{:S(2)}) collective-permute-start(bf16[48,1024]{1,0:T(8,128)(2,1)S(1)} %get-tuple-element.24), channel_id=1, source_target_pairs={{0,3},{1,2},{2,1},{3,0},{4,7},{5,6},{6,5},{7,4},{8,11},{9,10},{10,... | collective-permute-start | bytes 294920 | tf_op jit(solution)/shard_map/ppermute | solution.py:31
  12.7 6.6 %collective-permute-done.5.refs_0_ = bf16[48,1024]{1,0:T(8,128)(2,1)S(1)} collective-permute-done((bf16[48,1024]{1,0:T(8,128)(2,1)S(1)}, bf16[48,1024]{1,0:T(8,128)(2,1)S(1)}, u32[]{:S(2)}, u32[]{:S(2)}) %collective-permute-start.5) | collective-permute-done | bytes 98336 | tf_op jit(solution)/shard_map/ppermute | solution.py:31
  19.3 0.5 %shard_map.100 = bf16[48,768]{1,0:T(8,128)(2,1)S(1)} custom-call(bf16[48,1024]{1,0:T(8,128)(2,1)S(1)} %collective-permute-done.5.refs_0_, bf16[768,1024]{1,0:T(8,128)(2,1)S(1)} %shard_map.96.refs_2_.refs_1_), custom_call_target="tpu_custom_call" | custom-call | flops 75497472 | bytes 1671168 | tf_op jit(solution)/shard_map/pallas_call | solution.py:49
  19.9 0.0 copy-start
  19.9 0.0 copy-start.2
  20.0 0.1 collective-permute-start.6
  20.0 0.5 %shard_map.101 = bf16[48,768]{1,0:T(8,128)(2,1)S(1)} custom-call(bf16[48,1024]{1,0:T(8,128)(2,1)S(1)} %collective-permute-done.8.refs_0_, bf16[768,1024]{1,0:T(8,128)(2,1)S(1)} %shard_map.96.refs_2_.refs_1_), custom_call_target="tpu_custom_call" | custom-call | flops 75497472 | bytes 1671168 | tf_op jit(solution)/shard_map/pallas_call | solution.py:49
  20.6 0.6 %collective-permute-start.9 = (bf16[48,768]{1,0:T(8,128)(2,1)S(1)}, bf16[48,768]{1,0:T(8,128)(2,1)S(1)}, u32[]{:S(2)}, u32[]{:S(2)}) collective-permute-start(bf16[48,768]{1,0:T(8,128)(2,1)S(1)} %shard_map.101), channel_id=1, source_target_pairs={{0,4},{1,5},{2,6},{3,7},{4,0},{5,1},{6,2},{7,3},{8,12},{9,13},{10,... | collective-permute-start | bytes 221192 | tf_op jit(solution)/shard_map/ppermute | solution.py:31
  21.2 1.8 %collective-permute-start.2 = (bf16[96,768]{1,0:T(8,128)(2,1)S(1)}, bf16[96,768]{1,0:T(8,128)(2,1)S(1)}, u32[]{:S(2)}, u32[]{:S(2)}) collective-permute-start(bf16[96,768]{1,0:T(8,128)(2,1)S(1)} %add_convert_fusion.here_ref), channel_id=1, source_target_pairs={{0,8},{1,9},{2,10},{3,11},{4,12},{5,13},{6,14},{7,15},{8,0},{9,1},... | collective-permute-start | bytes 442376 | tf_op jit(solution)/shard_map/ppermute | solution.py:31
  23.0 0.9 %collective-permute-start.10 = (bf16[48,768]{1,0:T(8,128)(2,1)S(1)}, bf16[48,768]{1,0:T(8,128)(2,1)S(1)}, u32[]{:S(2)}, u32[]{:S(2)}) collective-permute-start(bf16[48,768]{1,0:T(8,128)(2,1)S(1)} %add_convert_fusion.1.here_ref), channel_id=1, source_target_pairs={{0,8},{1,9},{2,10},{3,11},{4,12},{5,13},{6,14},{7,15},{8,0},{9,1},... | collective-permute-start | bytes 221192 | tf_op jit(solution)/shard_map/ppermute | solution.py:31
  23.9 3.9 %collective-permute-done.2.other_ref = bf16[96,768]{1,0:T(8,128)(2,1)S(1)} collective-permute-done((bf16[96,768]{1,0:T(8,128)(2,1)S(1)}, bf16[96,768]{1,0:T(8,128)(2,1)S(1)}, u32[]{:S(2)}, u32[]{:S(2)}) %collective-permute-start.2) | collective-permute-done | bytes 147488 | tf_op jit(solution)/shard_map/ppermute | solution.py:31
  27.9 1.1 %shard_map.98 = (bf16[48,1024]{1,0:T(8,128)(2,1)S(1)}, bf16[48,128]{1,0:T(8,128)(2,1)S(1)}, bf16[48,1152]{1,0:T(8,128)(2,1)S(1)}) custom-call(bf16[96,768]{1,0:T(8,128)(2,1)S(1)} %add_convert_fusion.here_ref, bf16[96,768]{1,0:T(8,128)(2,1)S(1)} %collective-permute-done.2.other_ref, bf16[4,48,768]{2,1,0:T(8,128)(2,1)S(1)} %bitcast.22, ...), custom_call_target="tpu_custom_call" | custom-call | flops 301989888 | bytes 4030464 | tf_op jit(solution)/shard_map/pallas_call | solution.py:49
  29.0 1.6 %collective-permute-start.3 = (bf16[48,1152]{1,0:T(8,128)(2,1)S(1)}, bf16[48,1152]{1,0:T(8,128)(2,1)S(1)}, u32[]{:S(2)}, u32[]{:S(2)}) collective-permute-start(bf16[48,1152]{1,0:T(8,128)(2,1)S(1)} %get-tuple-element.21), channel_id=1, source_target_pairs={{0,1},{1,0},{2,3},{3,2},{4,5},{5,4},{6,7},{7,6},{8,9},{9,8},{10,11... | collective-permute-start | bytes 331784 | tf_op jit(solution)/shard_map/ppermute | solution.py:31
  30.6 1.6 %collective-permute-start.7 = (bf16[48,768]{1,0:T(8,128)(2,1)S(1)}, bf16[48,768]{1,0:T(8,128)(2,1)S(1)}, u32[]{:S(2)}, u32[]{:S(2)}) collective-permute-start(bf16[48,768]{1,0:T(8,128)(2,1)S(1)} %add_convert_fusion.2.here_ref), channel_id=1, source_target_pairs={{0,8},{1,9},{2,10},{3,11},{4,12},{5,13},{6,14},{7,15},{8,0},{9,1},... | collective-permute-start | bytes 221192 | tf_op jit(solution)/shard_map/ppermute | solution.py:31
  32.2 1.7 %collective-permute-done.3.refs_0_.refs_3_ = bf16[48,1152]{1,0:T(8,128)(2,1)S(1)} collective-permute-done((bf16[48,1152]{1,0:T(8,128)(2,1)S(1)}, bf16[48,1152]{1,0:T(8,128)(2,1)S(1)}, u32[]{:S(2)}, u32[]{:S(2)}) %collective-permute-start.3) | collective-permute-done | bytes 110624 | tf_op jit(solution)/shard_map/ppermute | solution.py:31
  33.9 0.2 shard_map.99
  34.1 1.8 %collective-permute-start.4 = (bf16[64,1120]{1,0:T(8,128)(2,1)S(1)}, bf16[64,1120]{1,0:T(8,128)(2,1)S(1)}, u32[]{:S(2)}, u32[]{:S(2)}) collective-permute-start(bf16[64,1120]{1,0:T(8,128)(2,1)S(1)} %shard_map.99), channel_id=1, source_target_pairs={{0,16},{1,17},{2,18},{3,19},{4,20},{5,21},{6,22},{7,23},{8,24},{9,... | collective-permute-start | bytes 430088 | tf_op jit(solution)/shard_map/ppermute | solution.py:31
  35.9 1.1 %shard_map.102 = (bf16[48,1024]{1,0:T(8,128)(2,1)S(1)}, bf16[48,128]{1,0:T(8,128)(2,1)S(1)}) custom-call(bf16[48,768]{1,0:T(8,128)(2,1)S(1)} %add_convert_fusion.1.here_ref, bf16[48,768]{1,0:T(8,128)(2,1)S(1)} %collective-permute-done.10.other_ref, bf16[4,48,768]{2,1,0:T(8,128)(2,1)S(1)} %bitcast.23, bf16[4,48,768]{2,1,0:T(8,128)(2,1)S(1)} %bitcast.26, ...), custom_call_target="tpu_custom_call" | custom-call | flops 150994944 | bytes 3883008 | tf_op jit(solution)/shard_map/pallas_call | solution.py:49
  37.0 1.1 %shard_map.103 = (bf16[48,1024]{1,0:T(8,128)(2,1)S(1)}, bf16[48,128]{1,0:T(8,128)(2,1)S(1)}) custom-call(bf16[48,768]{1,0:T(8,128)(2,1)S(1)} %add_convert_fusion.2.here_ref, bf16[48,768]{1,0:T(8,128)(2,1)S(1)} %collective-permute-done.7.other_ref, bf16[4,48,768]{2,1,0:T(8,128)(2,1)S(1)} %bitcast.24, bf16[4,48,768]{2,1,0:T(8,128)(2,1)S(1)} %bitcast.27, ...), custom_call_target="tpu_custom_call" | custom-call | flops 150994944 | bytes 3895296 | tf_op jit(solution)/shard_map/pallas_call | solution.py:49
  38.1 3.2 %collective-permute-start.11 = (bf16[48,1024]{1,0:T(8,128)(2,1)S(1)}, bf16[48,1024]{1,0:T(8,128)(2,1)S(1)}, u32[]{:S(2)}, u32[]{:S(2)}) collective-permute-start(bf16[48,1024]{1,0:T(8,128)(2,1)S(1)} %get-tuple-element.26), channel_id=1, source_target_pairs={{0,18},{1,19},{2,16},{3,17},{4,22},{5,23},{6,20},{7,21},{8,26},{9,... | collective-permute-start | bytes 294920 | tf_op jit(solution)/shard_map/ppermute | solution.py:31
  41.2 1.4 %collective-permute-start.12 = (bf16[48,1024]{1,0:T(8,128)(2,1)S(1)}, bf16[48,1024]{1,0:T(8,128)(2,1)S(1)}, u32[]{:S(2)}, u32[]{:S(2)}) collective-permute-start(bf16[48,1024]{1,0:T(8,128)(2,1)S(1)} %get-tuple-element.27), channel_id=1, source_target_pairs={{0,19},{1,18},{2,17},{3,16},{4,23},{5,22},{6,21},{7,20},{8,27},{9,... | collective-permute-start | bytes 294920 | tf_op jit(solution)/shard_map/ppermute | solution.py:31
  42.6 3.4 %collective-permute-start.13 = (bf16[48,128]{1,0:T(8,128)(2,1)S(1)}, bf16[48,128]{1,0:T(8,128)(2,1)S(1)}, u32[]{:S(2)}, u32[]{:S(2)}) collective-permute-start(bf16[48,128]{1,0:T(8,128)(2,1)S(1)} %get-tuple-element.29), channel_id=1, source_target_pairs={{0,3},{1,2},{2,1},{3,0},{4,6},{5,7},{6,4},{7,5},{8,11},{9,10},{10,... | collective-permute-start | bytes 36872 | tf_op jit(solution)/shard_map/ppermute | solution.py:31
  46.0 2.7 %collective-permute-done.13.refs_4_ = bf16[48,128]{1,0:T(8,128)(2,1)S(1)} collective-permute-done((bf16[48,128]{1,0:T(8,128)(2,1)S(1)}, bf16[48,128]{1,0:T(8,128)(2,1)S(1)}, u32[]{:S(2)}, u32[]{:S(2)}) %collective-permute-start.13) | collective-permute-done | bytes 12320 | tf_op jit(solution)/shard_map/ppermute | solution.py:31
  48.8 1.2 %collective-permute-done.14.refs_5_ = bf16[48,128]{1,0:T(8,128)(2,1)S(1)} collective-permute-done((bf16[48,128]{1,0:T(8,128)(2,1)S(1)}, bf16[48,128]{1,0:T(8,128)(2,1)S(1)}, u32[]{:S(2)}, u32[]{:S(2)}) %collective-permute-start.14) | collective-permute-done | bytes 12320 | tf_op jit(solution)/shard_map/ppermute | solution.py:31
  49.9 0.9 %shard_map.104 = (bf16[64,1024]{1,0:T(8,128)(2,1)}, bf16[2,64]{1,0:T(2,128)(2,1)}) custom-call(bf16[64,1120]{1,0:T(8,128)(2,1)S(1)} %collective-permute-done.4.message_ref, bf16[2,192,64]{2,1,0:T(8,128)(2,1)S(1)} %get-tuple-element.22.hold_ref, bf16[48,1024]{1,0:T(8,128)(2,1)S(1)} %collective-permute-done.11.refs_0_, ...), custom_call_target="tpu_custom_call" | custom-call | flops 12582912 | bytes 536576 | tf_op jit(solution)/shard_map/pallas_call | solution.py:49
  (21 shorter events, 0.1 us)
Async XLA Ops:
  1.9 5.9 %collective-permute-start = (bf16[48,1024]{1,0:T(8,128)(2,1)S(1)}, bf16[48,1024]{1,0:T(8,128)(2,1)S(1)}, u32[]{:S(2)}, u32[]{:S(2)}) collective-permute-start(bf16[48,1024]{1,0:T(8,128)(2,1)S(1)} %get-tuple-element.19), channel_id=1, source_target_pairs={{0,1},{1,0},{2,3},{3,2},{4,5},{5,4},{6,7},{7,6},{8,9},{9,8},{10,11... | collective-permute-start | bytes 294920 | tf_op jit(solution)/shard_map/ppermute | solution.py:31
  8.4 12.8 %collective-permute-start.1 = (bf16[96,768]{1,0:T(8,128)(2,1)S(1)}, bf16[96,768]{1,0:T(8,128)(2,1)S(1)}, u32[]{:S(2)}, u32[]{:S(2)}) collective-permute-start(bf16[96,768]{1,0:T(8,128)(2,1)S(1)} %shard_map.97), channel_id=1, source_target_pairs={{0,4},{1,5},{2,6},{3,7},{4,0},{5,1},{6,2},{7,3},{8,12},{9,13},{10,... | collective-permute-start | bytes 442376 | tf_op jit(solution)/shard_map/ppermute | solution.py:31
  8.5 10.8 %collective-permute-start.5 = (bf16[48,1024]{1,0:T(8,128)(2,1)S(1)}, bf16[48,1024]{1,0:T(8,128)(2,1)S(1)}, u32[]{:S(2)}, u32[]{:S(2)}) collective-permute-start(bf16[48,1024]{1,0:T(8,128)(2,1)S(1)} %get-tuple-element.23), channel_id=1, source_target_pairs={{0,2},{1,3},{2,0},{3,1},{4,6},{5,7},{6,4},{7,5},{8,10},{9,11},{10,... | collective-permute-start | bytes 294920 | tf_op jit(solution)/shard_map/ppermute | solution.py:31
  11.4 8.6 %collective-permute-start.8 = (bf16[48,1024]{1,0:T(8,128)(2,1)S(1)}, bf16[48,1024]{1,0:T(8,128)(2,1)S(1)}, u32[]{:S(2)}, u32[]{:S(2)}) collective-permute-start(bf16[48,1024]{1,0:T(8,128)(2,1)S(1)} %get-tuple-element.24), channel_id=1, source_target_pairs={{0,3},{1,2},{2,1},{3,0},{4,7},{5,6},{6,5},{7,4},{8,11},{9,10},{10,... | collective-permute-start | bytes 294920 | tf_op jit(solution)/shard_map/ppermute | solution.py:31
  19.3 8.5 %copy-start.1 = (bf16[1,1,1024,768]{3,2,1,0:T(8,128)(2,1)S(1)}, bf16[1,1,1024,768]{3,2,1,0:T(8,128)(2,1)}, u32[]{:S(2)}) copy-start(bf16[1,1,1024,768]{3,2,1,0:T(8,128)(2,1)} %param.12) | copy-start | bytes 4718596
  19.9 7.9 %copy-start = (bf16[1,1,1024,768]{3,2,1,0:T(8,128)(2,1)S(1)}, bf16[1,1,1024,768]{3,2,1,0:T(8,128)(2,1)}, u32[]{:S(2)}) copy-start(bf16[1,1,1024,768]{3,2,1,0:T(8,128)(2,1)} %param.11) | copy-start | bytes 4718596
  19.9 7.9 %copy-start.2 = (bf16[1,1,4,48,768]{4,3,2,1,0:T(8,128)(2,1)S(1)}, bf16[1,1,4,48,768]{4,3,2,1,0:T(8,128)(2,1)}, u32[]{:S(2)}) copy-start(bf16[1,1,4,48,768]{4,3,2,1,0:T(8,128)(2,1)} %param.14) | copy-start | bytes 884740
  19.9 7.9 %copy-start.3 = (bf16[1,1,4,48,768]{4,3,2,1,0:T(8,128)(2,1)S(1)}, bf16[1,1,4,48,768]{4,3,2,1,0:T(8,128)(2,1)}, u32[]{:S(2)}) copy-start(bf16[1,1,4,48,768]{4,3,2,1,0:T(8,128)(2,1)} %param.15) | copy-start | bytes 884740
  20.0 10.7 %collective-permute-start.6 = (bf16[48,768]{1,0:T(8,128)(2,1)S(1)}, bf16[48,768]{1,0:T(8,128)(2,1)S(1)}, u32[]{:S(2)}, u32[]{:S(2)}) collective-permute-start(bf16[48,768]{1,0:T(8,128)(2,1)S(1)} %shard_map.100), channel_id=1, source_target_pairs={{0,4},{1,5},{2,6},{3,7},{4,0},{5,1},{6,2},{7,3},{8,12},{9,13},{10,... | collective-permute-start | bytes 221192 | tf_op jit(solution)/shard_map/ppermute | solution.py:31
  20.6 2.4 %collective-permute-start.9 = (bf16[48,768]{1,0:T(8,128)(2,1)S(1)}, bf16[48,768]{1,0:T(8,128)(2,1)S(1)}, u32[]{:S(2)}, u32[]{:S(2)}) collective-permute-start(bf16[48,768]{1,0:T(8,128)(2,1)S(1)} %shard_map.101), channel_id=1, source_target_pairs={{0,4},{1,5},{2,6},{3,7},{4,0},{5,1},{6,2},{7,3},{8,12},{9,13},{10,... | collective-permute-start | bytes 221192 | tf_op jit(solution)/shard_map/ppermute | solution.py:31
  21.2 6.6 %collective-permute-start.2 = (bf16[96,768]{1,0:T(8,128)(2,1)S(1)}, bf16[96,768]{1,0:T(8,128)(2,1)S(1)}, u32[]{:S(2)}, u32[]{:S(2)}) collective-permute-start(bf16[96,768]{1,0:T(8,128)(2,1)S(1)} %add_convert_fusion.here_ref), channel_id=1, source_target_pairs={{0,8},{1,9},{2,10},{3,11},{4,12},{5,13},{6,14},{7,15},{8,0},{9,1},... | collective-permute-start | bytes 442376 | tf_op jit(solution)/shard_map/ppermute | solution.py:31
  23.0 12.9 %collective-permute-start.10 = (bf16[48,768]{1,0:T(8,128)(2,1)S(1)}, bf16[48,768]{1,0:T(8,128)(2,1)S(1)}, u32[]{:S(2)}, u32[]{:S(2)}) collective-permute-start(bf16[48,768]{1,0:T(8,128)(2,1)S(1)} %add_convert_fusion.1.here_ref), channel_id=1, source_target_pairs={{0,8},{1,9},{2,10},{3,11},{4,12},{5,13},{6,14},{7,15},{8,0},{9,1},... | collective-permute-start | bytes 221192 | tf_op jit(solution)/shard_map/ppermute | solution.py:31
  27.9 6.0 %copy-start.4 = (bf16[1,64,1024]{2,1,0:T(8,128)(2,1)S(1)}, bf16[1,64,1024]{2,1,0:T(8,128)(2,1)}, u32[]{:S(2)}) copy-start(bf16[1,64,1024]{2,1,0:T(8,128)(2,1)} %param.8) | copy-start | bytes 393220
  29.0 4.8 %collective-permute-start.3 = (bf16[48,1152]{1,0:T(8,128)(2,1)S(1)}, bf16[48,1152]{1,0:T(8,128)(2,1)S(1)}, u32[]{:S(2)}, u32[]{:S(2)}) collective-permute-start(bf16[48,1152]{1,0:T(8,128)(2,1)S(1)} %get-tuple-element.21), channel_id=1, source_target_pairs={{0,1},{1,0},{2,3},{3,2},{4,5},{5,4},{6,7},{7,6},{8,9},{9,8},{10,11... | collective-permute-start | bytes 331784 | tf_op jit(solution)/shard_map/ppermute | solution.py:31
  30.6 6.4 %collective-permute-start.7 = (bf16[48,768]{1,0:T(8,128)(2,1)S(1)}, bf16[48,768]{1,0:T(8,128)(2,1)S(1)}, u32[]{:S(2)}, u32[]{:S(2)}) collective-permute-start(bf16[48,768]{1,0:T(8,128)(2,1)S(1)} %add_convert_fusion.2.here_ref), channel_id=1, source_target_pairs={{0,8},{1,9},{2,10},{3,11},{4,12},{5,13},{6,14},{7,15},{8,0},{9,1},... | collective-permute-start | bytes 221192 | tf_op jit(solution)/shard_map/ppermute | solution.py:31
  34.1 15.9 %collective-permute-start.4 = (bf16[64,1120]{1,0:T(8,128)(2,1)S(1)}, bf16[64,1120]{1,0:T(8,128)(2,1)S(1)}, u32[]{:S(2)}, u32[]{:S(2)}) collective-permute-start(bf16[64,1120]{1,0:T(8,128)(2,1)S(1)} %shard_map.99), channel_id=1, source_target_pairs={{0,16},{1,17},{2,18},{3,19},{4,20},{5,21},{6,22},{7,23},{8,24},{9,... | collective-permute-start | bytes 430088 | tf_op jit(solution)/shard_map/ppermute | solution.py:31
  38.1 11.9 %collective-permute-start.11 = (bf16[48,1024]{1,0:T(8,128)(2,1)S(1)}, bf16[48,1024]{1,0:T(8,128)(2,1)S(1)}, u32[]{:S(2)}, u32[]{:S(2)}) collective-permute-start(bf16[48,1024]{1,0:T(8,128)(2,1)S(1)} %get-tuple-element.26), channel_id=1, source_target_pairs={{0,18},{1,19},{2,16},{3,17},{4,22},{5,23},{6,20},{7,21},{8,26},{9,... | collective-permute-start | bytes 294920 | tf_op jit(solution)/shard_map/ppermute | solution.py:31
  41.2 8.7 %collective-permute-start.12 = (bf16[48,1024]{1,0:T(8,128)(2,1)S(1)}, bf16[48,1024]{1,0:T(8,128)(2,1)S(1)}, u32[]{:S(2)}, u32[]{:S(2)}) collective-permute-start(bf16[48,1024]{1,0:T(8,128)(2,1)S(1)} %get-tuple-element.27), channel_id=1, source_target_pairs={{0,19},{1,18},{2,17},{3,16},{4,23},{5,22},{6,21},{7,20},{8,27},{9,... | collective-permute-start | bytes 294920 | tf_op jit(solution)/shard_map/ppermute | solution.py:31
  42.6 6.1 %collective-permute-start.13 = (bf16[48,128]{1,0:T(8,128)(2,1)S(1)}, bf16[48,128]{1,0:T(8,128)(2,1)S(1)}, u32[]{:S(2)}, u32[]{:S(2)}) collective-permute-start(bf16[48,128]{1,0:T(8,128)(2,1)S(1)} %get-tuple-element.29), channel_id=1, source_target_pairs={{0,3},{1,2},{2,1},{3,0},{4,6},{5,7},{6,4},{7,5},{8,11},{9,10},{10,... | collective-permute-start | bytes 36872 | tf_op jit(solution)/shard_map/ppermute | solution.py:31
  48.8 1.2 %collective-permute-start.14 = (bf16[48,128]{1,0:T(8,128)(2,1)S(1)}, bf16[48,128]{1,0:T(8,128)(2,1)S(1)}, u32[]{:S(2)}, u32[]{:S(2)}) collective-permute-start(bf16[48,128]{1,0:T(8,128)(2,1)S(1)} %collective-permute-done.13.refs_4_), channel_id=1, source_target_pairs={{0,4},{1,5},{2,6},{3,7},{4,0},{5,1},{6,2},{7,3},{8,12},{9,13},{10,... | collective-permute-start | bytes 36872 | tf_op jit(solution)/shard_map/ppermute | solution.py:31

commit v4 on v3

--- a/solution.py
+++ b/solution.py
@@ -57,17 +57,7 @@
     )(*ins)
 
 
-def table_kernel(capacity, experts, route_hbm, gate_hbm, grads_hbm, *refs):
-    row_refs, (gated_ref, hold_ref) = (refs[:experts], refs[experts : experts + 2])
-    route_ref, gate_ref, grads_ref, semaphores = refs[experts + 2 :]
-    copies = [
-        pltpu.make_async_copy(source, target, semaphores.at[index])
-        for index, (source, target) in enumerate(
-            ((route_hbm, route_ref), (gate_hbm, gate_ref), (grads_hbm, grads_ref))
-        )
-    ]
-    for copy in copies:
-        copy.start()
+def slot_tables(capacity, experts, route_ref):
     picks, tokens = route_ref.shape
     slots = experts * capacity
     place = lax.broadcasted_iota(jnp.int32, (slots, 1), 0)
@@ -77,30 +67,53 @@
     row = lax.broadcasted_iota(jnp.int32, (tokens, tokens), 0)
     column = lax.broadcasted_iota(jnp.int32, (tokens, tokens), 1)
     before = jnp.where(row < column, 1.0, 0.0).astype(jnp.bfloat16)
-    copies[0].wait()
     named = [route_ref[pick : pick + 1, :] == label for pick in range(picks)]
     names = functools.reduce(jnp.logical_or, named)
     earlier = matmul(jnp.where(names, 1.0, 0.0).astype(jnp.bfloat16), before)
-    fits = earlier == inside
+    return named, names, earlier == inside
+
+
+def copy_all(sources, targets, semaphores):
+    copies = [
+        pltpu.make_async_copy(source, target, semaphores.at[index])
+        for index, (source, target) in enumerate(zip(sources, targets))
+    ]
+    for copy in copies:
+        copy.start()
+    return copies
+
+
+def table_kernel(capacity, experts, route_hbm, grads_hbm, *refs):
+    row_refs, (route_ref, grads_ref, semaphores) = (refs[:experts], refs[experts:])
+    copies = copy_all((route_hbm, grads_hbm), (route_ref, grads_ref), semaphores)
+    copies[0].wait()
+    _, names, fits = slot_tables(capacity, experts, route_ref)
     placed = jnp.where(names & fits, 1.0, 0.0).astype(jnp.bfloat16)
-    copies[2].wait()
-    for k, ref in enumerate(row_refs):
-        ref[...] = matmul(placed[k * capacity : (k + 1) * capacity], grads_ref[...]).astype(
-            jnp.bfloat16
-        )
     copies[1].wait()
-    gated = jnp.zeros((slots, tokens), jnp.float32)
+    width = grads_ref.shape[1]
+    tile = 256 if width % 256 == 0 else width
+    for start in range(0, width, tile):
+        part = pl.ds(start, tile)
+        rows = matmul(placed, grads_ref[:, part]).astype(jnp.bfloat16)
+        for k, ref in enumerate(row_refs):
+            ref[:, part] = rows[k * capacity : (k + 1) * capacity]
+
+
+def fetch_kernel(capacity, experts, route_hbm, gate_hbm, down_hbm, gated_ref, hold_ref, down_ref, route_ref, gate_ref, semaphores):
+    copies = copy_all(
+        (route_hbm, gate_hbm, down_hbm), (route_ref, gate_ref, down_ref), semaphores
+    )
+    picks, tokens = route_ref.shape
+    copies[0].wait()
+    named, _, fits = slot_tables(capacity, experts, route_ref)
+    copies[1].wait()
+    gated = jnp.zeros((experts * capacity, tokens), jnp.float32)
     for pick in range(picks):
         here = jnp.where(named[pick] & fits, 1.0, 0.0)
         hold_ref[pick] = here.astype(jnp.bfloat16)
         gated = gated + here * gate_ref[pick : pick + 1, :].astype(jnp.float32)
     gated_ref[...] = gated.astype(jnp.bfloat16)
-
-
-def fetch_kernel(source_ref, target_ref, semaphore):
-    copy = pltpu.make_async_copy(source_ref, target_ref, semaphore)
-    copy.start()
-    copy.wait()
+    copies[2].wait()
 
 
 def raw_kernel(*refs):
@@ -110,23 +123,29 @@
 
 
 def back_kernel(offsets, capacity, name, here_ref, other_ref, saved_gate_ref, saved_up_ref, gate_ref, up_ref, *refs):
-    total = here_ref[...].astype(jnp.float32) + other_ref[...].astype(jnp.float32)
-
-    def picked(ref):
-        return jnp.concatenate([ref[lax.axis_index("expert") ^ k] for k in offsets]).astype(jnp.float32)
-
-    gate_val, up_val = (picked(saved_gate_ref), picked(saved_up_ref))
-    sigmoid_val = jax.nn.sigmoid(gate_val)
-    silu_val = gate_val * sigmoid_val
-    hidden = (silu_val * up_val).astype(jnp.bfloat16).astype(jnp.float32)
-    inner = jnp.sum(hidden * total, axis=1, keepdims=True)
-    gate_back = (
-        total * up_val * sigmoid_val * (1.0 + gate_val * (1.0 - sigmoid_val))
-    ).astype(jnp.bfloat16)
-    up_back = (total * silu_val).astype(jnp.bfloat16)
-    back = (matmul_t(gate_back, gate_ref[...]) + matmul_t(up_back, up_ref[...])).astype(
-        jnp.bfloat16
-    )
+    units = here_ref.shape[1]
+    step = 256 if units % 256 == 0 else units
+    inner, back = (0.0, 0.0)
+    for start in range(0, units, step):
+        part = pl.ds(start, step)
+        total = here_ref[:, part].astype(jnp.float32) + other_ref[:, part].astype(jnp.float32)
+
+        def picked(ref):
+            return jnp.concatenate(
+                [ref[lax.axis_index("expert") ^ k, :, part] for k in offsets]
+            ).astype(jnp.float32)
+
+        gate_val, up_val = (picked(saved_gate_ref), picked(saved_up_ref))
+        sigmoid_val = jax.nn.sigmoid(gate_val)
+        silu_val = gate_val * sigmoid_val
+        hidden = (silu_val * up_val).astype(jnp.bfloat16).astype(jnp.float32)
+        inner = inner + jnp.sum(hidden * total, axis=1, keepdims=True)
+        gate_back = (
+            total * up_val * sigmoid_val * (1.0 + gate_val * (1.0 - sigmoid_val))
+        ).astype(jnp.bfloat16)
+        up_back = (total * silu_val).astype(jnp.bfloat16)
+        back = back + matmul_t(gate_back, gate_ref[:, part]) + matmul_t(up_back, up_ref[:, part])
+    back = back.astype(jnp.bfloat16)
     inner = jnp.broadcast_to(inner, (inner.shape[0], 128)).astype(jnp.bfloat16)
     count = len(offsets)
     if name == "b":
@@ -201,21 +220,16 @@
     units = w_down.shape[2]
     bf16 = lambda *shape: jax.ShapeDtypeStruct(shape, jnp.bfloat16)
 
-    *rows, gated, holds = kernel_call(
+    rows = kernel_call(
         functools.partial(table_kernel, capacity, experts),
-        (
-            *[bf16(capacity, width)] * experts,
-            bf16(experts * capacity, tokens),
-            bf16(picks, experts * capacity, tokens),
-        ),
-        (route_block.T, gate_weights[0].T, grads_here),
+        (bf16(capacity, width),) * experts,
+        (route_block.T, grads_here),
         2 * experts * capacity * tokens * width,
-        [pltpu.HBM] * 3,
+        [pltpu.HBM] * 2,
         (
             pltpu.VMEM((picks, tokens), jnp.int32),
-            pltpu.VMEM((picks, tokens), jnp.bfloat16),
             pltpu.VMEM((tokens, width), jnp.bfloat16),
-            pltpu.SemaphoreType.DMA((3,)),
+            pltpu.SemaphoreType.DMA((2,)),
         ),
     )
 
@@ -235,13 +249,21 @@
                 arrived[k] = moved(rows[k], across(k))
 
     gate, up, gate_pre, up_pre = (w_gate[0, 0], w_up[0, 0], saved_gate[0, 0], saved_up[0, 0])
-    down = kernel_call(
-        fetch_kernel,
-        bf16(units, width),
-        (w_down[0, 0],),
+    gated, holds, down = kernel_call(
+        functools.partial(fetch_kernel, capacity, experts),
+        (
+            bf16(experts * capacity, tokens),
+            bf16(picks, experts * capacity, tokens),
+            bf16(units, width),
+        ),
+        (route_block.T, gate_weights[0].T, w_down[0, 0]),
         0,
-        [pltpu.HBM],
-        (pltpu.SemaphoreType.DMA,),
+        [pltpu.HBM] * 3,
+        (
+            pltpu.VMEM((picks, tokens), jnp.int32),
+            pltpu.VMEM((picks, tokens), jnp.bfloat16),
+            pltpu.SemaphoreType.DMA((3,)),
+        ),
     )
     row_grad, slot_grad = ({}, {})
     for name in ("c", "a", "b"):

time: 51 us -> 50.9 us (level)
  no operation moved by 1% of the time
where the time goes in v4:
time: 50.9 us; the launch traced here: 50.7 us
  starting transfers between devices  23.7 us (47%)
  waiting for transfers between devices  17.4 us (34%)
  Pallas kernels  8.69 us (17%)
  between operations  0.82 us (2%)
    ppermute x15, starting transfers between devices, moved(): return lax.ppermute(value, AXES, device_pairs(route))  23.7 us
    ppermute x15, waiting for transfers between devices, moved(): return lax.ppermute(value, AXES, device_pairs(route))  17.4 us
    pallas_call x10, Pallas kernels, kernel_call(): pl.pallas_call(body, out_shape=outs, in_specs=[pl.BlockSpec(memory_space=...  8.69 us
  transfers between devices with their start and end apart: 15, of which 6 were waited for; matrix products, arithmetic and copies ran while one was open for 0% of the time, Pallas kernels for 12%

profile of v4, /device:TPU:0, one launch (start us, length us, event | category | flops | bytes accessed | tf_op | source)
XLA Modules:
  0.0 50.7 jit_solution(13582934143004791020)
XLA Ops:
  0.6 1.2 %shard_map.96 = (bf16[48,1024]{1,0:T(8,128)(2,1)S(1)}, bf16[48,1024]{1,0:T(8,128)(2,1)S(1)}, bf16[48,1024]{1,0:T(8,128)(2,1)S(1)}, bf16[48,1024]{1,0:T(8,128)(2,1)S(1)}) custom-call(s32[2,64]{1,0:T(2,128)} %bitcast.31, bf16[64,1024]{1,0:T(8,128)(2,1)} %bitcast.28), custom_call_target="tpu_custom_call" | custom-call | flops 25165824 | bytes 131584 | tf_op jit(solution)/shard_map/pallas_call | solution.py:49
  1.8 3.1 %collective-permute-start = (bf16[48,1024]{1,0:T(8,128)(2,1)S(1)}, bf16[48,1024]{1,0:T(8,128)(2,1)S(1)}, u32[]{:S(2)}, u32[]{:S(2)}) collective-permute-start(bf16[48,1024]{1,0:T(8,128)(2,1)S(1)} %get-tuple-element.20), channel_id=1, source_target_pairs={{0,1},{1,0},{2,3},{3,2},{4,5},{5,4},{6,7},{7,6},{8,9},{9,8},{10,11... | collective-permute-start | bytes 294920 | tf_op jit(solution)/shard_map/ppermute | solution.py:31
  4.9 1.5 %shard_map.95 = (bf16[192,64]{1,0:T(8,128)(2,1)S(1)}, bf16[2,192,64]{2,1,0:T(8,128)(2,1)S(1)}, bf16[768,1024]{1,0:T(8,128)(2,1)S(1)}) custom-call(s32[2,64]{1,0:T(2,128)} %bitcast.32, bf16[2,64]{1,0:T(2,128)(2,1)} %bitcast.33, bf16[768,1024]{1,0:T(8,128)(2,1)} %bitcast.30), custom_call_target="tpu_custom_call" | custom-call | bytes 1573632 | tf_op jit(solution)/shard_map/pallas_call | solution.py:49
  6.4 1.3 %collective-permute-done.refs_1_ = bf16[48,1024]{1,0:T(8,128)(2,1)S(1)} collective-permute-done((bf16[48,1024]{1,0:T(8,128)(2,1)S(1)}, bf16[48,1024]{1,0:T(8,128)(2,1)S(1)}, u32[]{:S(2)}, u32[]{:S(2)}) %collective-permute-start) | collective-permute-done | bytes 98336 | tf_op jit(solution)/shard_map/ppermute | solution.py:31
  7.7 0.6 %shard_map.97 = bf16[96,768]{1,0:T(8,128)(2,1)S(1)} custom-call(bf16[48,1024]{1,0:T(8,128)(2,1)S(1)} %get-tuple-element.19.refs_0_, bf16[48,1024]{1,0:T(8,128)(2,1)S(1)} %collective-permute-done.refs_1_, bf16[768,1024]{1,0:T(8,128)(2,1)S(1)} %get-tuple-element.21.refs_2_.refs_1_), custom_call_target="tpu_custom_call" | custom-call | flops 150994944 | bytes 1769472 | tf_op jit(solution)/shard_map/pallas_call | solution.py:49
  8.3 0.1 collective-permute-start.1
  8.4 2.9 %collective-permute-start.5 = (bf16[48,1024]{1,0:T(8,128)(2,1)S(1)}, bf16[48,1024]{1,0:T(8,128)(2,1)S(1)}, u32[]{:S(2)}, u32[]{:S(2)}) collective-permute-start(bf16[48,1024]{1,0:T(8,128)(2,1)S(1)} %get-tuple-element.25), channel_id=1, source_target_pairs={{0,2},{1,3},{2,0},{3,1},{4,6},{5,7},{6,4},{7,5},{8,10},{9,11},{10,... | collective-permute-start | bytes 294920 | tf_op jit(solution)/shard_map/ppermute | solution.py:31
  11.3 1.4 %collective-permute-start.8 = (bf16[48,1024]{1,0:T(8,128)(2,1)S(1)}, bf16[48,1024]{1,0:T(8,128)(2,1)S(1)}, u32[]{:S(2)}, u32[]{:S(2)}) collective-permute-start(bf16[48,1024]{1,0:T(8,128)(2,1)S(1)} %get-tuple-element.26), channel_id=1, source_target_pairs={{0,3},{1,2},{2,1},{3,0},{4,7},{5,6},{6,5},{7,4},{8,11},{9,10},{10,... | collective-permute-start | bytes 294920 | tf_op jit(solution)/shard_map/ppermute | solution.py:31
  12.7 6.6 %collective-permute-done.5.refs_0_ = bf16[48,1024]{1,0:T(8,128)(2,1)S(1)} collective-permute-done((bf16[48,1024]{1,0:T(8,128)(2,1)S(1)}, bf16[48,1024]{1,0:T(8,128)(2,1)S(1)}, u32[]{:S(2)}, u32[]{:S(2)}) %collective-permute-start.5) | collective-permute-done | bytes 98336 | tf_op jit(solution)/shard_map/ppermute | solution.py:31
  19.3 0.5 %shard_map.100 = bf16[48,768]{1,0:T(8,128)(2,1)S(1)} custom-call(bf16[48,1024]{1,0:T(8,128)(2,1)S(1)} %collective-permute-done.5.refs_0_, bf16[768,1024]{1,0:T(8,128)(2,1)S(1)} %get-tuple-element.21.refs_2_.refs_1_), custom_call_target="tpu_custom_call" | custom-call | flops 75497472 | bytes 1671168 | tf_op jit(solution)/shard_map/pallas_call | solution.py:49
  19.8 0.0 copy-start
  19.9 0.1 collective-permute-start.6
  20.0 0.5 %shard_map.101 = bf16[48,768]{1,0:T(8,128)(2,1)S(1)} custom-call(bf16[48,1024]{1,0:T(8,128)(2,1)S(1)} %collective-permute-done.8.refs_0_, bf16[768,1024]{1,0:T(8,128)(2,1)S(1)} %get-tuple-element.21.refs_2_.refs_1_), custom_call_target="tpu_custom_call" | custom-call | flops 75497472 | bytes 1671168 | tf_op jit(solution)/shard_map/pallas_call | solution.py:49
  20.5 0.6 %collective-permute-start.9 = (bf16[48,768]{1,0:T(8,128)(2,1)S(1)}, bf16[48,768]{1,0:T(8,128)(2,1)S(1)}, u32[]{:S(2)}, u32[]{:S(2)}) collective-permute-start(bf16[48,768]{1,0:T(8,128)(2,1)S(1)} %shard_map.101), channel_id=1, source_target_pairs={{0,4},{1,5},{2,6},{3,7},{4,0},{5,1},{6,2},{7,3},{8,12},{9,13},{10,... | collective-permute-start | bytes 221192 | tf_op jit(solution)/shard_map/ppermute | solution.py:31
  21.1 1.8 %collective-permute-start.2 = (bf16[96,768]{1,0:T(8,128)(2,1)S(1)}, bf16[96,768]{1,0:T(8,128)(2,1)S(1)}, u32[]{:S(2)}, u32[]{:S(2)}) collective-permute-start(bf16[96,768]{1,0:T(8,128)(2,1)S(1)} %add_convert_fusion.here_ref), channel_id=1, source_target_pairs={{0,8},{1,9},{2,10},{3,11},{4,12},{5,13},{6,14},{7,15},{8,0},{9,1},... | collective-permute-start | bytes 442376 | tf_op jit(solution)/shard_map/ppermute | solution.py:31
  23.0 0.9 %collective-permute-start.10 = (bf16[48,768]{1,0:T(8,128)(2,1)S(1)}, bf16[48,768]{1,0:T(8,128)(2,1)S(1)}, u32[]{:S(2)}, u32[]{:S(2)}) collective-permute-start(bf16[48,768]{1,0:T(8,128)(2,1)S(1)} %add_convert_fusion.1.here_ref), channel_id=1, source_target_pairs={{0,8},{1,9},{2,10},{3,11},{4,12},{5,13},{6,14},{7,15},{8,0},{9,1},... | collective-permute-start | bytes 221192 | tf_op jit(solution)/shard_map/ppermute | solution.py:31
  23.8 3.9 %collective-permute-done.2.other_ref = bf16[96,768]{1,0:T(8,128)(2,1)S(1)} collective-permute-done((bf16[96,768]{1,0:T(8,128)(2,1)S(1)}, bf16[96,768]{1,0:T(8,128)(2,1)S(1)}, u32[]{:S(2)}, u32[]{:S(2)}) %collective-permute-start.2) | collective-permute-done | bytes 147488 | tf_op jit(solution)/shard_map/ppermute | solution.py:31
  27.8 0.0 copy-start.4
  27.8 1.1 %shard_map.98 = (bf16[48,1024]{1,0:T(8,128)(2,1)S(1)}, bf16[48,128]{1,0:T(8,128)(2,1)S(1)}, bf16[48,1152]{1,0:T(8,128)(2,1)S(1)}) custom-call(bf16[96,768]{1,0:T(8,128)(2,1)S(1)} %add_convert_fusion.here_ref, bf16[96,768]{1,0:T(8,128)(2,1)S(1)} %collective-permute-done.2.other_ref, bf16[4,48,768]{2,1,0:T(8,128)(2,1)S(1)} %bitcast.22, ...), custom_call_target="tpu_custom_call" | custom-call | flops 301989888 | bytes 4030464 | tf_op jit(solution)/shard_map/pallas_call | solution.py:49
  28.9 1.6 %collective-permute-start.3 = (bf16[48,1152]{1,0:T(8,128)(2,1)S(1)}, bf16[48,1152]{1,0:T(8,128)(2,1)S(1)}, u32[]{:S(2)}, u32[]{:S(2)}) collective-permute-start(bf16[48,1152]{1,0:T(8,128)(2,1)S(1)} %get-tuple-element.23), channel_id=1, source_target_pairs={{0,1},{1,0},{2,3},{3,2},{4,5},{5,4},{6,7},{7,6},{8,9},{9,8},{10,11... | collective-permute-start | bytes 331784 | tf_op jit(solution)/shard_map/ppermute | solution.py:31
  30.5 1.6 %collective-permute-start.7 = (bf16[48,768]{1,0:T(8,128)(2,1)S(1)}, bf16[48,768]{1,0:T(8,128)(2,1)S(1)}, u32[]{:S(2)}, u32[]{:S(2)}) collective-permute-start(bf16[48,768]{1,0:T(8,128)(2,1)S(1)} %add_convert_fusion.2.here_ref), channel_id=1, source_target_pairs={{0,8},{1,9},{2,10},{3,11},{4,12},{5,13},{6,14},{7,15},{8,0},{9,1},... | collective-permute-start | bytes 221192 | tf_op jit(solution)/shard_map/ppermute | solution.py:31
  32.1 1.6 %collective-permute-done.3.refs_0_.refs_3_ = bf16[48,1152]{1,0:T(8,128)(2,1)S(1)} collective-permute-done((bf16[48,1152]{1,0:T(8,128)(2,1)S(1)}, bf16[48,1152]{1,0:T(8,128)(2,1)S(1)}, u32[]{:S(2)}, u32[]{:S(2)}) %collective-permute-start.3) | collective-permute-done | bytes 110624 | tf_op jit(solution)/shard_map/ppermute | solution.py:31
  33.8 0.2 shard_map.99
  34.0 1.8 %collective-permute-start.4 = (bf16[64,1120]{1,0:T(8,128)(2,1)S(1)}, bf16[64,1120]{1,0:T(8,128)(2,1)S(1)}, u32[]{:S(2)}, u32[]{:S(2)}) collective-permute-start(bf16[64,1120]{1,0:T(8,128)(2,1)S(1)} %shard_map.99), channel_id=1, source_target_pairs={{0,16},{1,17},{2,18},{3,19},{4,20},{5,21},{6,22},{7,23},{8,24},{9,... | collective-permute-start | bytes 430088 | tf_op jit(solution)/shard_map/ppermute | solution.py:31
  35.8 1.0 %shard_map.102 = (bf16[48,1024]{1,0:T(8,128)(2,1)S(1)}, bf16[48,128]{1,0:T(8,128)(2,1)S(1)}) custom-call(bf16[48,768]{1,0:T(8,128)(2,1)S(1)} %add_convert_fusion.1.here_ref, bf16[48,768]{1,0:T(8,128)(2,1)S(1)} %collective-permute-done.10.other_ref, bf16[4,48,768]{2,1,0:T(8,128)(2,1)S(1)} %bitcast.23, bf16[4,48,768]{2,1,0:T(8,128)(2,1)S(1)} %bitcast.26, ...), custom_call_target="tpu_custom_call" | custom-call | flops 150994944 | bytes 3883008 | tf_op jit(solution)/shard_map/pallas_call | solution.py:49
  36.9 1.0 %shard_map.103 = (bf16[48,1024]{1,0:T(8,128)(2,1)S(1)}, bf16[48,128]{1,0:T(8,128)(2,1)S(1)}) custom-call(bf16[48,768]{1,0:T(8,128)(2,1)S(1)} %add_convert_fusion.2.here_ref, bf16[48,768]{1,0:T(8,128)(2,1)S(1)} %collective-permute-done.7.other_ref, bf16[4,48,768]{2,1,0:T(8,128)(2,1)S(1)} %bitcast.24, bf16[4,48,768]{2,1,0:T(8,128)(2,1)S(1)} %bitcast.27, ...), custom_call_target="tpu_custom_call" | custom-call | flops 150994944 | bytes 3895296 | tf_op jit(solution)/shard_map/pallas_call | solution.py:49
  37.9 3.2 %collective-permute-start.11 = (bf16[48,1024]{1,0:T(8,128)(2,1)S(1)}, bf16[48,1024]{1,0:T(8,128)(2,1)S(1)}, u32[]{:S(2)}, u32[]{:S(2)}) collective-permute-start(bf16[48,1024]{1,0:T(8,128)(2,1)S(1)} %get-tuple-element.28), channel_id=1, source_target_pairs={{0,18},{1,19},{2,16},{3,17},{4,22},{5,23},{6,20},{7,21},{8,26},{9,... | collective-permute-start | bytes 294920 | tf_op jit(solution)/shard_map/ppermute | solution.py:31
  41.1 1.4 %collective-permute-start.12 = (bf16[48,1024]{1,0:T(8,128)(2,1)S(1)}, bf16[48,1024]{1,0:T(8,128)(2,1)S(1)}, u32[]{:S(2)}, u32[]{:S(2)}) collective-permute-start(bf16[48,1024]{1,0:T(8,128)(2,1)S(1)} %get-tuple-element.29), channel_id=1, source_target_pairs={{0,19},{1,18},{2,17},{3,16},{4,23},{5,22},{6,21},{7,20},{8,27},{9,... | collective-permute-start | bytes 294920 | tf_op jit(solution)/shard_map/ppermute | solution.py:31
  42.5 3.4 %collective-permute-start.13 = (bf16[48,128]{1,0:T(8,128)(2,1)S(1)}, bf16[48,128]{1,0:T(8,128)(2,1)S(1)}, u32[]{:S(2)}, u32[]{:S(2)}) collective-permute-start(bf16[48,128]{1,0:T(8,128)(2,1)S(1)} %get-tuple-element.31), channel_id=1, source_target_pairs={{0,3},{1,2},{2,1},{3,0},{4,6},{5,7},{6,4},{7,5},{8,11},{9,10},{10,... | collective-permute-start | bytes 36872 | tf_op jit(solution)/shard_map/ppermute | solution.py:31
  45.9 2.7 %collective-permute-done.13.refs_4_ = bf16[48,128]{1,0:T(8,128)(2,1)S(1)} collective-permute-done((bf16[48,128]{1,0:T(8,128)(2,1)S(1)}, bf16[48,128]{1,0:T(8,128)(2,1)S(1)}, u32[]{:S(2)}, u32[]{:S(2)}) %collective-permute-start.13) | collective-permute-done | bytes 12320 | tf_op jit(solution)/shard_map/ppermute | solution.py:31
  48.6 1.2 %collective-permute-done.14.refs_5_ = bf16[48,128]{1,0:T(8,128)(2,1)S(1)} collective-permute-done((bf16[48,128]{1,0:T(8,128)(2,1)S(1)}, bf16[48,128]{1,0:T(8,128)(2,1)S(1)}, u32[]{:S(2)}, u32[]{:S(2)}) %collective-permute-start.14) | collective-permute-done | bytes 12320 | tf_op jit(solution)/shard_map/ppermute | solution.py:31
  49.8 0.9 %shard_map.104 = (bf16[64,1024]{1,0:T(8,128)(2,1)}, bf16[2,64]{1,0:T(2,128)(2,1)}) custom-call(bf16[64,1120]{1,0:T(8,128)(2,1)S(1)} %collective-permute-done.4.message_ref, bf16[2,192,64]{2,1,0:T(8,128)(2,1)S(1)} %get-tuple-element.24.hold_ref, bf16[48,1024]{1,0:T(8,128)(2,1)S(1)} %collective-permute-done.11.refs_0_, ...), custom_call_target="tpu_custom_call" | custom-call | flops 12582912 | bytes 536576 | tf_op jit(solution)/shard_map/pallas_call | solution.py:49
  (21 shorter events, 0.1 us)
Async XLA Ops:
  1.8 5.9 %collective-permute-start = (bf16[48,1024]{1,0:T(8,128)(2,1)S(1)}, bf16[48,1024]{1,0:T(8,128)(2,1)S(1)}, u32[]{:S(2)}, u32[]{:S(2)}) collective-permute-start(bf16[48,1024]{1,0:T(8,128)(2,1)S(1)} %get-tuple-element.20), channel_id=1, source_target_pairs={{0,1},{1,0},{2,3},{3,2},{4,5},{5,4},{6,7},{7,6},{8,9},{9,8},{10,11... | collective-permute-start | bytes 294920 | tf_op jit(solution)/shard_map/ppermute | solution.py:31
  8.3 12.8 %collective-permute-start.1 = (bf16[96,768]{1,0:T(8,128)(2,1)S(1)}, bf16[96,768]{1,0:T(8,128)(2,1)S(1)}, u32[]{:S(2)}, u32[]{:S(2)}) collective-permute-start(bf16[96,768]{1,0:T(8,128)(2,1)S(1)} %shard_map.97), channel_id=1, source_target_pairs={{0,4},{1,5},{2,6},{3,7},{4,0},{5,1},{6,2},{7,3},{8,12},{9,13},{10,... | collective-permute-start | bytes 442376 | tf_op jit(solution)/shard_map/ppermute | solution.py:31
  8.4 10.8 %collective-permute-start.5 = (bf16[48,1024]{1,0:T(8,128)(2,1)S(1)}, bf16[48,1024]{1,0:T(8,128)(2,1)S(1)}, u32[]{:S(2)}, u32[]{:S(2)}) collective-permute-start(bf16[48,1024]{1,0:T(8,128)(2,1)S(1)} %get-tuple-element.25), channel_id=1, source_target_pairs={{0,2},{1,3},{2,0},{3,1},{4,6},{5,7},{6,4},{7,5},{8,10},{9,11},{10,... | collective-permute-start | bytes 294920 | tf_op jit(solution)/shard_map/ppermute | solution.py:31
  11.3 8.6 %collective-permute-start.8 = (bf16[48,1024]{1,0:T(8,128)(2,1)S(1)}, bf16[48,1024]{1,0:T(8,128)(2,1)S(1)}, u32[]{:S(2)}, u32[]{:S(2)}) collective-permute-start(bf16[48,1024]{1,0:T(8,128)(2,1)S(1)} %get-tuple-element.26), channel_id=1, source_target_pairs={{0,3},{1,2},{2,1},{3,0},{4,7},{5,6},{6,5},{7,4},{8,11},{9,10},{10,... | collective-permute-start | bytes 294920 | tf_op jit(solution)/shard_map/ppermute | solution.py:31
  19.3 8.5 %copy-start.1 = (bf16[1,1,1024,768]{3,2,1,0:T(8,128)(2,1)S(1)}, bf16[1,1,1024,768]{3,2,1,0:T(8,128)(2,1)}, u32[]{:S(2)}) copy-start(bf16[1,1,1024,768]{3,2,1,0:T(8,128)(2,1)} %param.12) | copy-start | bytes 4718596
  19.8 7.9 %copy-start = (bf16[1,1,1024,768]{3,2,1,0:T(8,128)(2,1)S(1)}, bf16[1,1,1024,768]{3,2,1,0:T(8,128)(2,1)}, u32[]{:S(2)}) copy-start(bf16[1,1,1024,768]{3,2,1,0:T(8,128)(2,1)} %param.11) | copy-start | bytes 4718596
  19.8 7.9 %copy-start.2 = (bf16[1,1,4,48,768]{4,3,2,1,0:T(8,128)(2,1)S(1)}, bf16[1,1,4,48,768]{4,3,2,1,0:T(8,128)(2,1)}, u32[]{:S(2)}) copy-start(bf16[1,1,4,48,768]{4,3,2,1,0:T(8,128)(2,1)} %param.14) | copy-start | bytes 884740
  19.9 7.9 %copy-start.3 = (bf16[1,1,4,48,768]{4,3,2,1,0:T(8,128)(2,1)S(1)}, bf16[1,1,4,48,768]{4,3,2,1,0:T(8,128)(2,1)}, u32[]{:S(2)}) copy-start(bf16[1,1,4,48,768]{4,3,2,1,0:T(8,128)(2,1)} %param.15) | copy-start | bytes 884740
  19.9 10.7 %collective-permute-start.6 = (bf16[48,768]{1,0:T(8,128)(2,1)S(1)}, bf16[48,768]{1,0:T(8,128)(2,1)S(1)}, u32[]{:S(2)}, u32[]{:S(2)}) collective-permute-start(bf16[48,768]{1,0:T(8,128)(2,1)S(1)} %shard_map.100), channel_id=1, source_target_pairs={{0,4},{1,5},{2,6},{3,7},{4,0},{5,1},{6,2},{7,3},{8,12},{9,13},{10,... | collective-permute-start | bytes 221192 | tf_op jit(solution)/shard_map/ppermute | solution.py:31
  20.5 2.4 %collective-permute-start.9 = (bf16[48,768]{1,0:T(8,128)(2,1)S(1)}, bf16[48,768]{1,0:T(8,128)(2,1)S(1)}, u32[]{:S(2)}, u32[]{:S(2)}) collective-permute-start(bf16[48,768]{1,0:T(8,128)(2,1)S(1)} %shard_map.101), channel_id=1, source_target_pairs={{0,4},{1,5},{2,6},{3,7},{4,0},{5,1},{6,2},{7,3},{8,12},{9,13},{10,... | collective-permute-start | bytes 221192 | tf_op jit(solution)/shard_map/ppermute | solution.py:31
  21.1 6.6 %collective-permute-start.2 = (bf16[96,768]{1,0:T(8,128)(2,1)S(1)}, bf16[96,768]{1,0:T(8,128)(2,1)S(1)}, u32[]{:S(2)}, u32[]{:S(2)}) collective-permute-start(bf16[96,768]{1,0:T(8,128)(2,1)S(1)} %add_convert_fusion.here_ref), channel_id=1, source_target_pairs={{0,8},{1,9},{2,10},{3,11},{4,12},{5,13},{6,14},{7,15},{8,0},{9,1},... | collective-permute-start | bytes 442376 | tf_op jit(solution)/shard_map/ppermute | solution.py:31
  23.0 12.9 %collective-permute-start.10 = (bf16[48,768]{1,0:T(8,128)(2,1)S(1)}, bf16[48,768]{1,0:T(8,128)(2,1)S(1)}, u32[]{:S(2)}, u32[]{:S(2)}) collective-permute-start(bf16[48,768]{1,0:T(8,128)(2,1)S(1)} %add_convert_fusion.1.here_ref), channel_id=1, source_target_pairs={{0,8},{1,9},{2,10},{3,11},{4,12},{5,13},{6,14},{7,15},{8,0},{9,1},... | collective-permute-start | bytes 221192 | tf_op jit(solution)/shard_map/ppermute | solution.py:31
  27.8 6.0 %copy-start.4 = (bf16[1,64,1024]{2,1,0:T(8,128)(2,1)S(1)}, bf16[1,64,1024]{2,1,0:T(8,128)(2,1)}, u32[]{:S(2)}) copy-start(bf16[1,64,1024]{2,1,0:T(8,128)(2,1)} %param.8) | copy-start | bytes 393220
  28.9 4.8 %collective-permute-start.3 = (bf16[48,1152]{1,0:T(8,128)(2,1)S(1)}, bf16[48,1152]{1,0:T(8,128)(2,1)S(1)}, u32[]{:S(2)}, u32[]{:S(2)}) collective-permute-start(bf16[48,1152]{1,0:T(8,128)(2,1)S(1)} %get-tuple-element.23), channel_id=1, source_target_pairs={{0,1},{1,0},{2,3},{3,2},{4,5},{5,4},{6,7},{7,6},{8,9},{9,8},{10,11... | collective-permute-start | bytes 331784 | tf_op jit(solution)/shard_map/ppermute | solution.py:31
  30.5 6.3 %collective-permute-start.7 = (bf16[48,768]{1,0:T(8,128)(2,1)S(1)}, bf16[48,768]{1,0:T(8,128)(2,1)S(1)}, u32[]{:S(2)}, u32[]{:S(2)}) collective-permute-start(bf16[48,768]{1,0:T(8,128)(2,1)S(1)} %add_convert_fusion.2.here_ref), channel_id=1, source_target_pairs={{0,8},{1,9},{2,10},{3,11},{4,12},{5,13},{6,14},{7,15},{8,0},{9,1},... | collective-permute-start | bytes 221192 | tf_op jit(solution)/shard_map/ppermute | solution.py:31
  34.0 15.8 %collective-permute-start.4 = (bf16[64,1120]{1,0:T(8,128)(2,1)S(1)}, bf16[64,1120]{1,0:T(8,128)(2,1)S(1)}, u32[]{:S(2)}, u32[]{:S(2)}) collective-permute-start(bf16[64,1120]{1,0:T(8,128)(2,1)S(1)} %shard_map.99), channel_id=1, source_target_pairs={{0,16},{1,17},{2,18},{3,19},{4,20},{5,21},{6,22},{7,23},{8,24},{9,... | collective-permute-start | bytes 430088 | tf_op jit(solution)/shard_map/ppermute | solution.py:31
  37.9 11.9 %collective-permute-start.11 = (bf16[48,1024]{1,0:T(8,128)(2,1)S(1)}, bf16[48,1024]{1,0:T(8,128)(2,1)S(1)}, u32[]{:S(2)}, u32[]{:S(2)}) collective-permute-start(bf16[48,1024]{1,0:T(8,128)(2,1)S(1)} %get-tuple-element.28), channel_id=1, source_target_pairs={{0,18},{1,19},{2,16},{3,17},{4,22},{5,23},{6,20},{7,21},{8,26},{9,... | collective-permute-start | bytes 294920 | tf_op jit(solution)/shard_map/ppermute | solution.py:31
  41.1 8.7 %collective-permute-start.12 = (bf16[48,1024]{1,0:T(8,128)(2,1)S(1)}, bf16[48,1024]{1,0:T(8,128)(2,1)S(1)}, u32[]{:S(2)}, u32[]{:S(2)}) collective-permute-start(bf16[48,1024]{1,0:T(8,128)(2,1)S(1)} %get-tuple-element.29), channel_id=1, source_target_pairs={{0,19},{1,18},{2,17},{3,16},{4,23},{5,22},{6,21},{7,20},{8,27},{9,... | collective-permute-start | bytes 294920 | tf_op jit(solution)/shard_map/ppermute | solution.py:31
  42.5 6.1 %collective-permute-start.13 = (bf16[48,128]{1,0:T(8,128)(2,1)S(1)}, bf16[48,128]{1,0:T(8,128)(2,1)S(1)}, u32[]{:S(2)}, u32[]{:S(2)}) collective-permute-start(bf16[48,128]{1,0:T(8,128)(2,1)S(1)} %get-tuple-element.31), channel_id=1, source_target_pairs={{0,3},{1,2},{2,1},{3,0},{4,6},{5,7},{6,4},{7,5},{8,11},{9,10},{10,... | collective-permute-start | bytes 36872 | tf_op jit(solution)/shard_map/ppermute | solution.py:31
  48.6 1.2 %collective-permute-start.14 = (bf16[48,128]{1,0:T(8,128)(2,1)S(1)}, bf16[48,128]{1,0:T(8,128)(2,1)S(1)}, u32[]{:S(2)}, u32[]{:S(2)}) collective-permute-start(bf16[48,128]{1,0:T(8,128)(2,1)S(1)} %collective-permute-done.13.refs_4_), channel_id=1, source_target_pairs={{0,4},{1,5},{2,6},{3,7},{4,0},{5,1},{6,2},{7,3},{8,12},{9,13},{10,... | collective-permute-start | bytes 36872 | tf_op jit(solution)/shard_map/ppermute | solution.py:31
